TPU v7x, 1024 devices: a whole 8x8x8 slice. The times are simulated.
1024 devices in a mesh: seq: 64 (over x_lo, z, core), chan: 16 (over y, x_hi).
Axes of the slice: x: 8 (x_hi: 2, x_lo: 4; x = x_hi * 4 + x_lo), y: 8, z: 8, core: 2. Of those that a mesh axis runs over, the one named last changes fastest.
Arguments:
- q_one: bfloat16 [8192, 8192], P('chan', 'seq'), may hold values from -6 to 6
- k_one: bfloat16 [8192, 8192], P('chan', 'seq'), may hold values from -6 to 6
- v_one: bfloat16 [8192, 8192], P('chan', 'seq'), may hold values from -6 to 6
- fir_taps: bfloat16 [8192, 128], P('chan'), may hold values from -0.5 to 0.5
- q_two: bfloat16 [8192, 8192], P('chan', 'seq'), may hold values from -6 to 6
- k_two: bfloat16 [8192, 8192], P('chan', 'seq'), may hold values from -6 to 6
- residues: float32 [8192, 16], P('chan'), may hold values from -0.0625 to 0.0625
- decays: float32 [8192, 16], P('chan'), may hold values from 3.0517578e-05 to 0.08
- skip_gain: float32 [8192], P('chan'), may hold values from 0.5 to 1.5
Outputs:
- layer_one: bfloat16 [8192, 8192], P('chan', 'seq')
- layer_two: bfloat16 [8192, 8192], P('chan', 'seq')
All inputs are finite; a program needn't handle non-finite values.
Results may differ from a plain program's by a relative error of at most 0.012.
Values may be sent and summed in bfloat16 or wider, within the bound.
No kernel may reach another device: no remote copies, remote signals or barrier semaphores. Data moves between devices by JAX's collectives and lax.ppermute only.
A program may use at most 32 MiB of HBM per device.

v0:
```python
import math

import jax
import jax.numpy as jnp
from jax import lax
from jax.sharding import PartitionSpec as P


def from_behind(value, axis, steps):
    count = lax.axis_size(axis)
    leading, last = (max(0, -steps), min(count, count - steps))
    return lax.ppermute(value, axis, [(source, source + steps) for source in range(leading, last)])


def causal_filter(signal, fir_kernel):
    kernel = fir_kernel[:, ::-1][:, None, :]
    result = lax.conv_general_dilated(
        signal[None],
        kernel,
        (1,),
        "VALID",
        dimension_numbers=("NCH", "OIH", "NCH"),
        feature_group_count=signal.shape[0],
        preferred_element_type=jnp.float32,
    )
    return result[0]


def angle_table(left_count, right_count, period):
    left_index = jnp.arange(left_count, dtype=jnp.int32)
    right_index = jnp.arange(right_count, dtype=jnp.int32)
    angles = (left_index[:, None] * right_index[None, :] % period).astype(jnp.float32) * (
        2.0 * math.pi / period
    )
    return (jnp.cos(angles), jnp.sin(angles))


def matmul_hp(form, left, right):
    return jnp.einsum(form, left, right, precision=lax.Precision.HIGHEST)


def long_convolution(signal, mode_res, mode_dec):
    chan_count, length = signal.shape
    total = 2 * length
    inner = 128
    outer = total // inner
    half_outer = outer // 2
    cos_one, sin_one = angle_table(outer, outer, outer)
    cos_two, sin_two = angle_table(inner, inner, inner)
    cos_twist, sin_twist = angle_table(outer, inner, total)

    def forward(values):
        shaped = values.reshape(chan_count, half_outer, inner)
        real_one = matmul_hp("cab,ak->ckb", shaped, cos_one[:half_outer])
        imag_one = -matmul_hp("cab,ak->ckb", shaped, sin_one[:half_outer])
        rot_real = real_one * cos_twist + imag_one * sin_twist
        rot_imag = imag_one * cos_twist - real_one * sin_twist
        spec_real = matmul_hp("ckb,bm->ckm", rot_real, cos_two) + matmul_hp(
            "ckb,bm->ckm", rot_imag, sin_two
        )
        spec_imag = matmul_hp("ckb,bm->ckm", rot_imag, cos_two) - matmul_hp(
            "ckb,bm->ckm", rot_real, sin_two
        )
        return (spec_real, spec_imag)

    time_axis = jnp.arange(length, dtype=jnp.float32)
    long_filter = jnp.zeros((chan_count, length), jnp.float32)
    for mode_index in range(mode_res.shape[1]):
        long_filter = long_filter + mode_res[:, mode_index, None] * jnp.exp(
            -mode_dec[:, mode_index, None] * time_axis[None, :]
        )
    data_real, data_imag = forward(signal.astype(jnp.float32))
    filt_real, filt_imag = forward(long_filter)
    prod_real = data_real * filt_real - data_imag * filt_imag
    prod_imag = data_real * filt_imag + data_imag * filt_real
    back_real = matmul_hp("ckm,mb->ckb", prod_real, cos_two) - matmul_hp(
        "ckm,mb->ckb", prod_imag, sin_two
    )
    back_imag = matmul_hp("ckm,mb->ckb", prod_real, sin_two) + matmul_hp(
        "ckm,mb->ckb", prod_imag, cos_two
    )
    turn_real = back_real * cos_twist - back_imag * sin_twist
    turn_imag = back_real * sin_twist + back_imag * cos_twist
    output = matmul_hp("ckb,ka->cab", turn_real, cos_one[:, :half_outer]) - matmul_hp(
        "ckb,ka->cab", turn_imag, sin_one[:, :half_outer]
    )
    convolved = (output / total).reshape(chan_count, length)
    return lax.optimization_barrier(convolved.astype(jnp.bfloat16))


def apply_gate(gate_rows, convolved, gain_rows, mixed_in):
    summed = convolved.astype(jnp.float32) + gain_rows[:, None] * mixed_in.astype(jnp.float32)
    return (gate_rows.astype(jnp.float32) * summed).astype(jnp.bfloat16)


def body(q_one, k_one, v_one, fir_taps, q_two, k_two, residues, decays, skip_gain):
    chan_local, row_count = q_one.shape
    tap_count = fir_taps.shape[1]
    product = (k_one.astype(jnp.float32) * v_one.astype(jnp.float32)).astype(jnp.bfloat16)
    previous = from_behind(product, "seq", 1)
    padded = jnp.concatenate([previous[:, 1:], product], axis=1)
    filtered = causal_filter(padded, fir_taps)
    layer_one = (q_one.astype(jnp.float32) * filtered).astype(jnp.bfloat16)
    mixed_in = (k_two.astype(jnp.float32) * layer_one.astype(jnp.float32)).astype(jnp.bfloat16)
    group_width = chan_local // lax.axis_size("seq")
    first_channel = lax.axis_index("seq") * group_width
    mode_res = lax.dynamic_slice_in_dim(residues, first_channel, group_width, 0)
    mode_dec = lax.dynamic_slice_in_dim(decays, first_channel, group_width, 0)
    regrouped, gate_rows = (
        lax.all_to_all(mixed_in, "seq", split_axis=0, concat_axis=1, tiled=True),
        lax.all_to_all(q_two, "seq", split_axis=0, concat_axis=1, tiled=True),
    )
    convolved = long_convolution(regrouped, mode_res, mode_dec)
    gain_rows = lax.dynamic_slice_in_dim(skip_gain, first_channel, group_width, 0)
    gated = apply_gate(gate_rows, convolved, gain_rows, regrouped)
    layer_two = lax.all_to_all(gated, "seq", split_axis=1, concat_axis=0, tiled=True)
    return (layer_one, layer_two)


def solution(mesh):
    return jax.shard_map(
        body,
        mesh=mesh,
        in_specs=(
            P("chan", "seq"),
            P("chan", "seq"),
            P("chan", "seq"),
            P("chan", None),
            P("chan", "seq"),
            P("chan", "seq"),
            P("chan", None),
            P("chan", None),
            P("chan"),
        ),
        out_specs=(P("chan", "seq"), P("chan", "seq")),
        check_vma=False,
    )
```

profile of v0, /device:TPU:112, one launch (start us, length us, event | category | flops | bytes accessed | tf_op | source)
XLA Modules:
  0.0 89.5 jit_solution(2570437784998783081)
XLA Ops:
  0.6 1.0 %multiply_convert_fusion.1 = bf16[512,128]{1,0:T(8,128)(2,1)S(1)} fusion(bf16[512,128]{1,0:T(8,128)(2,1)} %param.11, bf16[512,128]{1,0:T(8,128)(2,1)} %param.10), kind=kLoop, calls=%fused_computation.51 | loop fusion | flops 262144 | bytes 393216 | tf_op jit(solution)/shard_map/convert_element_type | solution.py:99
  1.6 1.7 %collective-permute-start = (bf16[512,128]{1,0:T(8,128)(2,1)S(1)}, bf16[512,128]{1,0:T(8,128)(2,1)S(1)}, u32[]{:S(2)}, u32[]{:S(2)}) collective-permute-start(bf16[512,128]{1,0:T(8,128)(2,1)S(1)} %multiply_convert_fusion.1), channel_id=1, source_target_pairs={{0,16},{16,32},{32,48},{48,64},{64,80},{80,96},{96,112},{112,128},... | collective-permute-start | bytes 393224 | tf_op jit(solution)/shard_map/ppermute | solution.py:12
  3.4 0.3 fusion.63
  3.7 0.3 fusion.64
  3.9 0.3 fusion.61
  4.2 1.3 %fusion.93 = (f32[8]{0:T(128)S(1)}, f32[8]{0:T(128)S(1)}, f32[8]{0:T(128)S(1)}, f32[8]{0:T(128)S(1)}, f32[8]{0:T(128)S(1)}, /*index=5*/f32[8]{0:T(128)S(1)}, f32...) fusion(f32[512,16]{0,1:T(8,128)} %param.16, ...), kind=kLoop, calls=%fused_computation.146 | loop fusion | flops 128 | bytes 2112 | tf_op jit(solution)/shard_map/mul | solution.py:70
  5.5 1.4 %convolution_negate_fusion = f32[128,8,128]{2,0,1:T(8,128)S(1)} fusion(f32[128,128]{1,0:T(8,128)S(1)} %fusion.63, f32[8]{0:T(128)S(1)} %get-tuple-element.43, f32[8]{0:T(128)S(1)} %get-tuple-element.44, f32[8]{0:T(128)S(1)} %get-tuple-element.29, f32[8]{0:T(128)S(1)} %get-tuple-element.58, f32[8]{0:T(128)S(1)} %get-tuple-element.30, ...), kind=kOutput, calls=%fused_computation | convolution fusion | flops 103874560 | bytes 606208 | tf_op jit(solution)/shard_map/cab,ak->ckb/dot_general | solution.py:39
  6.9 1.4 %fusion.77 = f32[128,8,128]{2,0,1:T(8,128)S(1)} fusion(f32[128,128]{1,0:T(8,128)S(1)} %fusion.64, f32[8]{0:T(128)S(1)} %get-tuple-element.43, f32[8]{0:T(128)S(1)} %get-tuple-element.44, f32[8]{0:T(128)S(1)} %get-tuple-element.29, f32[8]{0:T(128)S(1)} %get-tuple-element.58, f32[8]{0:T(128)S(1)} %get-tuple-element.30, f32[8]{0:T(128)S(1)} %get-tuple-element.57, ...), kind=kOutput, calls=%fused_computation.99 | convolution fusion | flops 103743488 | bytes 606208 | tf_op jit(solution)/shard_map/cab,ak->ckb/dot_general | solution.py:39
  8.2 0.8 fusion.3
  9.1 0.8 convolution_subtract_fusion.1
  9.9 0.0 copy-start
  9.9 0.8 fusion.7
  10.7 0.1 copy-done
  10.8 0.4 rev.3
  11.2 0.0 copy-start.1
  11.2 0.9 copy.31
  12.1 0.0 copy-done.1
  12.1 0.0 copy-start.2
  12.1 0.1 copy.29
  12.2 0.8 copy-done.2
  13.0 0.1 copy.32
  13.1 0.8 dynamic_slice.11
  13.9 0.0 collective-permute-done
  13.9 0.1 slice.154
  14.0 0.1 maximum_bitcast_fusion
  14.1 0.6 copy.30
  14.7 5.8 %fusion.143 = f32[1,512,128]{1,0,2:T(1,128)S(1)} fusion(bf16[1,512,255]{1,0,2:T(2,128)(2,1)S(1)} %copy.30, bf16[512,1,128]{0,1,2:T(2,128)(2,1)} %copy.31), kind=kOutput, calls=%fused_computation.196 | convolution fusion | flops 16777216 | bytes 654336 | tf_op jit(solution)/shard_map/conv_general_dilated | solution.py:17
  20.5 0.1 multiply_convert_fusion
  20.6 0.8 copy.33
  21.4 21.8 %all-to-all-start.1 = ((bf16[64,8,128]{2,1,0:T(8,128)(2,1)}), bf16[64,8,128]{2,1,0:T(8,128)(2,1)S(1)}, u32[]{:S(2)}, u32[]{:S(2)}) async-start(bf16[64,8,128]{2,1,0:T(8,128)(2,1)} %bitcast.7), calls=%async_computation.1 | async-start | bytes 262144 | tf_op jit(solution)/shard_map/all_to_all | solution.py:110
  43.2 0.8 convolution_add_fusion.1
  44.0 9.6 %all-to-all-done.1 = bf16[64,8,128]{2,1,0:T(8,128)(2,1)S(1)} async-done(((bf16[64,8,128]{2,1,0:T(8,128)(2,1)}), bf16[64,8,128]{2,1,0:T(8,128)(2,1)S(1)}, u32[]{:S(2)}, u32[]{:S(2)}) %all-to-all-start.1) | async-done | bytes 131104 | tf_op jit(solution)/shard_map/all_to_all | solution.py:110
  53.6 4.8 %all-to-all-start = ((bf16[64,8,128]{2,1,0:T(8,128)(2,1)}), bf16[64,8,128]{2,1,0:T(8,128)(2,1)S(1)}, u32[]{:S(2)}, u32[]{:S(2)}) async-start(bf16[64,8,128]{2,1,0:T(8,128)(2,1)} %bitcast.2), calls=%async_computation | async-start | bytes 262144 | tf_op jit(solution)/shard_map/all_to_all | solution.py:111
  58.4 0.4 convolution_negate_fusion.1
  58.9 0.4 fusion.32
  59.3 0.8 fusion.13
  60.1 0.8 fusion.9
  60.9 0.8 convolution_add_fusion.2
  61.8 0.9 multiply_add_fusion
  62.6 0.8 fusion.48
  63.5 0.8 fusion.40
  64.3 0.8 convolution_subtract_fusion
  65.1 0.8 convolution_add_fusion
  65.9 0.5 fusion.18
  66.4 0.5 fusion.2
  67.0 0.1 copy.60
  67.1 1.6 %all-to-all-done = bf16[64,8,128]{2,1,0:T(8,128)(2,1)S(1)} async-done(((bf16[64,8,128]{2,1,0:T(8,128)(2,1)}), bf16[64,8,128]{2,1,0:T(8,128)(2,1)S(1)}, u32[]{:S(2)}, u32[]{:S(2)}) %all-to-all-start) | async-done | bytes 131104 | tf_op jit(solution)/shard_map/all_to_all | solution.py:111
  68.7 0.8 fusion.30
  69.5 9.0 %all-to-all-start.2 = ((bf16[8,64,128]{2,0,1:T(8,128)(2,1)}), bf16[8,64,128]{2,0,1:T(8,128)(2,1)S(1)}, u32[]{:S(2)}, u32[]{:S(2)}) async-start(bf16[8,64,128]{2,0,1:T(8,128)(2,1)} %fusion.30), calls=%async_computation.2 | async-start | bytes 262144 | tf_op jit(solution)/shard_map/all_to_all | solution.py:116
  78.5 0.8 copy.37
  79.2 9.7 %all-to-all-done.2 = bf16[8,64,128]{2,0,1:T(8,128)(2,1)S(1)} async-done(((bf16[8,64,128]{2,0,1:T(8,128)(2,1)}), bf16[8,64,128]{2,0,1:T(8,128)(2,1)S(1)}, u32[]{:S(2)}, u32[]{:S(2)}) %all-to-all-start.2) | async-done | bytes 131104 | tf_op jit(solution)/shard_map/all_to_all | solution.py:116
  88.9 0.7 copy.62
  (2 shorter events, 0.0 us)
Async XLA Ops:
  1.6 12.2 %collective-permute-start = (bf16[512,128]{1,0:T(8,128)(2,1)S(1)}, bf16[512,128]{1,0:T(8,128)(2,1)S(1)}, u32[]{:S(2)}, u32[]{:S(2)}) collective-permute-start(bf16[512,128]{1,0:T(8,128)(2,1)S(1)} %multiply_convert_fusion.1), channel_id=1, source_target_pairs={{0,16},{16,32},{32,48},{48,64},{64,80},{80,96},{96,112},{112,128},... | collective-permute-start | bytes 393224 | tf_op jit(solution)/shard_map/ppermute | solution.py:12
  9.9 0.9 %copy-start = (bf16[512,128]{1,0:T(8,128)(2,1)S(1)}, bf16[512,128]{1,0:T(8,128)(2,1)}, u32[]{:S(2)}) copy-start(bf16[512,128]{1,0:T(8,128)(2,1)} %param.12) | copy-start | bytes 393220
  11.2 0.9 %copy-start.1 = (bf16[512,128]{1,0:T(8,128)(2,1)S(1)}, bf16[512,128]{1,0:T(8,128)(2,1)}, u32[]{:S(2)}) copy-start(bf16[512,128]{1,0:T(8,128)(2,1)} %param.9) | copy-start | bytes 393220
  12.1 0.9 %copy-start.2 = (bf16[512,128]{1,0:T(8,128)(2,1)S(1)}, bf16[512,128]{1,0:T(8,128)(2,1)}, u32[]{:S(2)}) copy-start(bf16[512,128]{1,0:T(8,128)(2,1)} %param.14) | copy-start | bytes 393220
  21.4 32.2 %all-to-all-start.1 = ((bf16[64,8,128]{2,1,0:T(8,128)(2,1)}), bf16[64,8,128]{2,1,0:T(8,128)(2,1)S(1)}, u32[]{:S(2)}, u32[]{:S(2)}) async-start(bf16[64,8,128]{2,1,0:T(8,128)(2,1)} %bitcast.7), calls=%async_computation.1 | async-start | bytes 262144 | tf_op jit(solution)/shard_map/all_to_all | solution.py:110
  53.6 15.0 %all-to-all-start = ((bf16[64,8,128]{2,1,0:T(8,128)(2,1)}), bf16[64,8,128]{2,1,0:T(8,128)(2,1)S(1)}, u32[]{:S(2)}, u32[]{:S(2)}) async-start(bf16[64,8,128]{2,1,0:T(8,128)(2,1)} %bitcast.2), calls=%async_computation | async-start | bytes 262144 | tf_op jit(solution)/shard_map/all_to_all | solution.py:111
  69.5 19.4 %all-to-all-start.2 = ((bf16[8,64,128]{2,0,1:T(8,128)(2,1)}), bf16[8,64,128]{2,0,1:T(8,128)(2,1)S(1)}, u32[]{:S(2)}, u32[]{:S(2)}) async-start(bf16[8,64,128]{2,0,1:T(8,128)(2,1)} %fusion.30), calls=%async_computation.2 | async-start | bytes 262144 | tf_op jit(solution)/shard_map/all_to_all | solution.py:116
where the time goes:
time: 90.9 us; the launch traced here: 89.5 us
  starting transfers between devices  37.3 us (41%)
  waiting for transfers between devices  20.8 us (23%)
  matrix products  20.3 us (22%)
  local copies, waits for them, and re-layouts  6.05 us (7%)
  other arithmetic  4.13 us (5%)
  between operations  0.94 us (1%)
    all_to_all x1, starting transfers between devices, body(): lax.all_to_all(mixed_in, 'seq', split_axis=0, concat_axis=1, tiled=True)  21.8 us
    dot_general x18, matrix products, matmul_hp(): return jnp.einsum(form, left, right, precision=lax.Precision.HIGHEST)  14.4 us
    all_to_all x1, waiting for transfers between devices, body(): lax.all_to_all(gated, 'seq', split_axis=1, concat_axis=0, tiled=True)  9.65 us
    all_to_all x1, waiting for transfers between devices, body(): lax.all_to_all(mixed_in, 'seq', split_axis=0, concat_axis=1, tiled=True)  9.59 us
    all_to_all x1, starting transfers between devices, body(): lax.all_to_all(gated, 'seq', split_axis=1, concat_axis=0, tiled=True)  8.98 us
    conv_general_dilated x1, matrix products, causal_filter(): lax.conv_general_dilated(signal[None], kernel, (1,), 'VALID', dimension_n...  5.84 us
    all_to_all x1, starting transfers between devices, body(): lax.all_to_all(q_two, 'seq', split_axis=0, concat_axis=1, tiled=True)  4.8 us
    unnamed x11, local copies, waits for them, and re-layouts  2.61 us
  transfers between devices with their start and end apart: 4, of which 3 were waited for; matrix products, arithmetic and copies ran while one was open for 22% of the time, Pallas kernels for 0%

commit v1 on v0

v1 whole, which is shorter than its diff:
```python
import jax
import jax.numpy as jnp
from jax import lax
from jax.experimental import pallas as pl
from jax.experimental.pallas import tpu as pltpu
from jax.sharding import Mesh, PartitionSpec as P

LANES = 128
ROWS = 8
F32 = jnp.float32
BF16 = jnp.bfloat16
NEAR = 8


def call(kernel, outs, scratch=()):
    return pl.pallas_call(kernel, out_shape=outs, scratch_shapes=list(scratch))


def array(dtype, *shape):
    return jax.ShapeDtypeStruct(shape, dtype)


def turned(block):
    return jnp.swapaxes(block.astype(F32), 0, 1)


def rows_of(ref, tile, first, count=ROWS):
    return ref[tile, pl.ds(first, count), :]


def spread(ref, tile, row):
    return jnp.broadcast_to(ref[tile, pl.ds(row, 1), :], (ROWS, LANES))


def product_kernel(k_ref, v_ref, out_ref):
    for tile in range(out_ref.shape[0]):
        part = pl.ds(tile * LANES, LANES)
        product = (k_ref[part, :].astype(F32) * v_ref[part, :].astype(F32)).astype(BF16)
        out_ref[tile] = turned(product).astype(BF16)


def own_taps(signal_ref, taps_ref, tile, blocks):
    sums = [jnp.zeros((ROWS, LANES), F32) for _ in range(blocks)]
    for offset in range(ROWS):
        shifted = [rows_of(signal_ref, tile, ROWS + ROWS * at - offset) for at in range(blocks)]
        for step in range(blocks):
            weight = spread(taps_ref, tile, ROWS * step + offset)
            for at in range(step, blocks):
                sums[at] = sums[at] + weight * shifted[at - step]
    return sums


def earlier_taps(sums, signal_ref, taps_ref, tile, blocks):
    sums = list(sums)
    for offset in range(ROWS):
        shifted = {
            at: rows_of(signal_ref, tile, ROWS * (blocks + at) - offset)
            for at in range(1 - blocks, 1 if offset else 0)
        }
        for step in range(blocks):
            weight = spread(taps_ref, tile, ROWS * step + offset)
            for at in range(blocks):
                if at - step in shifted:
                    sums[at] = sums[at] + weight * shifted[at - step]
    return sums


def decayed_sums(starts, decay, blocks):
    out = []
    for at in range(blocks):
        terms = list(starts)
        while len(terms) > 1:
            terms = [a + b for a, b in zip(terms[::2], terms[1::2])]
        out.append(terms[0])
        if at + 1 < blocks:
            starts = [a * b for a, b in zip(starts, decay)]
    return out


def prepare_kernel(
    product_ref, taps_ref, q_ref, k_ref, res_ref, dec_ref,
    taps_out, part_out, q_out, k_out, filter_out, mode_out,
    signal_ref,
):
    tiles, length = product_ref.shape[0], product_ref.shape[1]
    blocks = length // ROWS
    modes = res_ref.shape[1]
    signal_ref[:, pl.ds(0, ROWS), :] = jnp.zeros((tiles, ROWS, LANES), F32)
    for tile in range(tiles):
        part = pl.ds(tile * LANES, LANES)
        signal_ref[tile, pl.ds(ROWS, length), :] = product_ref[tile].astype(F32)
        taps_out[tile] = turned(taps_ref[part, :])
        q_out[tile] = turned(q_ref[part, :])
        k_out[tile] = turned(k_ref[part, :])
        mode_out[tile, pl.ds(0, modes), :] = jnp.swapaxes(res_ref[part, :], 0, 1)
        mode_out[tile, pl.ds(modes, modes), :] = jnp.swapaxes(dec_ref[part, :], 0, 1)

    place = lax.broadcasted_iota(jnp.int32, (ROWS, LANES), 0).astype(F32)

    def one_tile(tile, carry):
        sums = own_taps(signal_ref, taps_out, tile, blocks)
        for at in range(blocks):
            part_out[tile, pl.ds(ROWS * at, ROWS), :] = sums[at]
        starts, decay = [], []
        for mode in range(modes):
            rate = spread(mode_out, tile, modes + mode)
            starts.append(spread(mode_out, tile, mode) * jnp.exp(-rate * place))
            decay.append(jnp.exp(-rate * float(ROWS)))
        for at, value in enumerate(decayed_sums(starts, decay, blocks)):
            filter_out[tile, pl.ds(ROWS * at, ROWS), :] = value
        return carry

    lax.fori_loop(0, tiles, one_tile, 0)


def mix_kernel(
    halo_ref, part_ref, taps_ref, q_ref, k_ref, mode_ref,
    one_out, mixed_out, state_out,
    signal_ref,
):
    tiles, length = part_ref.shape[0], part_ref.shape[1]
    blocks = length // ROWS
    modes = mode_ref.shape[1] // 2
    signal_ref[:, pl.ds(length, ROWS), :] = jnp.zeros((tiles, ROWS, LANES), F32)
    for tile in range(tiles):
        signal_ref[tile, pl.ds(0, length), :] = halo_ref[tile].astype(F32)

    left = (ROWS - 1 - lax.broadcasted_iota(jnp.int32, (ROWS, LANES), 0)).astype(F32)

    def one_tile(tile, carry):
        sums = [rows_of(part_ref, tile, ROWS * at) for at in range(blocks)]
        sums = earlier_taps(sums, signal_ref, taps_ref, tile, blocks)
        mixed = []
        for at in range(blocks):
            rows = pl.ds(ROWS * at, ROWS)
            first = (q_ref[tile, rows, :] * sums[at]).astype(BF16).astype(F32)
            mixed.append((k_ref[tile, rows, :] * first).astype(BF16).astype(F32))
            one_out[tile, rows, :] = first
            mixed_out[tile, rows, :] = mixed[-1]
        found = []
        for mode in range(modes):
            rate = spread(mode_ref, tile, modes + mode)
            decay = jnp.exp(-rate * float(ROWS))
            held = mixed[0]
            for at in range(1, blocks):
                held = held * decay + mixed[at]
            found.append(jnp.sum(held * jnp.exp(-rate * left), axis=0, keepdims=True))
        state = jnp.concatenate(found, axis=0).astype(BF16)
        for peer in range(NEAR):
            state_out[peer, pl.ds(pl.multiple_of(tile * modes, modes), modes), :] = state
        return carry

    lax.fori_loop(0, tiles, one_tile, 0)


def local_kernel(mixed_ref, filter_ref, one_ref, conv_out, one_out, signal_ref):
    tiles, length = mixed_ref.shape[0], mixed_ref.shape[1]
    blocks = length // ROWS
    signal_ref[:, pl.ds(0, ROWS), :] = jnp.zeros((tiles, ROWS, LANES), F32)
    for tile in range(tiles):
        signal_ref[tile, pl.ds(ROWS, length), :] = mixed_ref[tile]
        one_out[pl.ds(tile * LANES, LANES), :] = turned(one_ref[tile]).astype(BF16)

    def one_tile(tile, carry):
        sums = own_taps(signal_ref, filter_ref, tile, blocks)
        for at in range(blocks):
            conv_out[tile, pl.ds(ROWS * at, ROWS), :] = sums[at]
        return carry

    lax.fori_loop(0, tiles, one_tile, 0)


def near_kernel(heard_ref, mode_ref, before_out, whole_out):
    tiles, modes = mode_ref.shape[0], mode_ref.shape[1] // 2
    length = float(LANES)
    me = lax.axis_index("near")
    for tile in range(tiles):
        part = pl.ds(tile * modes, modes)
        step = jnp.exp(-mode_ref[tile, pl.ds(modes, modes), :] * length)
        before = jnp.zeros((modes, LANES), F32)
        whole = jnp.zeros((modes, LANES), F32)
        for peer in range(NEAR):
            state = heard_ref[peer, part, :].astype(F32)
            whole = whole * step + state
            before = jnp.where(peer < me, whole, before)
        before_out[part, :] = before
        for peer in range(whole_out.shape[0]):
            whole_out[peer, part, :] = whole.astype(BF16)


def finish_kernel(heard_ref, before_ref, mode_ref, conv_ref, mixed_ref, gate_ref, gain_ref, out_ref):
    tiles, length = mixed_ref.shape[0], mixed_ref.shape[1]
    blocks = length // ROWS
    modes = mode_ref.shape[1] // 2
    me, group = lax.axis_index("near"), lax.axis_index("far")
    skipped = (me * length).astype(F32)
    after = (1 + lax.broadcasted_iota(jnp.int32, (ROWS, LANES), 0)).astype(F32)
    for tile in range(tiles):
        part = pl.ds(tile * modes, modes)
        rates = mode_ref[tile, pl.ds(modes, modes), :]
        step = jnp.exp(-rates * float(length * NEAR))
        far = jnp.zeros((modes, LANES), F32)
        for peer in range(heard_ref.shape[0] - 1):
            far = jnp.where(peer < group, far * step + heard_ref[peer, part, :].astype(F32), far)
        entering = (before_ref[part, :] + far * jnp.exp(-rates * skipped)) * mode_ref[tile, pl.ds(0, modes), :]
        starts, decay = [], []
        for mode in range(modes):
            rate = jnp.broadcast_to(rates[mode : mode + 1, :], (ROWS, LANES))
            starts.append(jnp.broadcast_to(entering[mode : mode + 1, :], (ROWS, LANES)) * jnp.exp(-rate * after))
            decay.append(jnp.exp(-rate * float(ROWS)))
        gain = jnp.broadcast_to(gain_ref[pl.ds(tile, 1), :], (ROWS, LANES))
        made = []
        for at, value in enumerate(decayed_sums(starts, decay, blocks)):
            rows = pl.ds(ROWS * at, ROWS)
            convolved = (conv_ref[tile, rows, :] + value).astype(BF16).astype(F32)
            made.append(convolved + gain * mixed_ref[tile, rows, :])
        channels = pl.ds(tile * LANES, LANES)
        summed = turned(jnp.concatenate(made, axis=0))
        out_ref[channels, :] = (gate_ref[channels, :].astype(F32) * summed).astype(BF16)


def body(q_one, k_one, v_one, fir_taps, q_two, k_two, residues, decays, skip_gain):
    channels, length = q_one.shape
    tiles, modes = channels // LANES, residues.shape[1]
    seq = ("far", "near")
    far_count = lax.axis_size("far")
    count = far_count * lax.axis_size("near")
    product = call(product_kernel, array(BF16, tiles, length, LANES))(k_one, v_one)
    halo = lax.ppermute(product, seq, [(at, at + 1) for at in range(count - 1)])
    wide = array(F32, tiles, length, LANES)
    padded = pltpu.VMEM((tiles, length + ROWS, LANES), F32)
    taps, part, q_turned, k_turned, long_taps, mode_rows = call(
        prepare_kernel,
        (wide, wide, wide, wide, wide, array(F32, tiles, 2 * modes, LANES)),
        (padded,),
    )(product, fir_taps, q_one, k_two, residues, decays)
    one_turned, mixed, state = call(
        mix_kernel,
        (wide, wide, array(BF16, NEAR, tiles * modes, LANES)),
        (padded,),
    )(halo, part, taps, q_turned, k_turned, mode_rows)
    heard = lax.all_to_all(state, "near", split_axis=0, concat_axis=0, tiled=True)
    conv, layer_one = call(
        local_kernel, (wide, array(BF16, channels, length)), (padded,)
    )(mixed, long_taps, one_turned)
    before, whole = call(
        near_kernel,
        (array(F32, tiles * modes, LANES), array(BF16, far_count, tiles * modes, LANES)),
    )(heard, mode_rows)
    far_heard = lax.all_to_all(whole, "far", split_axis=0, concat_axis=0, tiled=True)
    layer_two = call(finish_kernel, array(BF16, channels, length))(
        far_heard, before, mode_rows, conv, mixed, q_two, skip_gain.reshape(tiles, LANES)
    )
    return (layer_one, layer_two)


def solution(mesh):
    count, chans = mesh.shape["seq"], mesh.shape["chan"]
    grid = Mesh(mesh.devices.reshape(count // NEAR, NEAR, chans), ("far", "near", "chan"))
    split = P("chan", ("far", "near"))
    whole = P("chan", None)
    return jax.shard_map(
        body,
        mesh=grid,
        in_specs=(split, split, split, whole, split, split, whole, whole, P("chan")),
        out_specs=(split, split),
        check_vma=False,
    )
```

time: 90.9 us -> 63.6 us (0.70)
  starting transfers between devices: 37.3 us -> 11.9 us
  blocking collectives: 0 us -> 21.2 us
  matrix products: 20.3 us -> 0 us
  Pallas kernels: 0 us -> 18.6 us
  waiting for transfers between devices: 20.8 us -> 7.75 us
  other arithmetic: 4.13 us -> 0 us
  local copies, waits for them, and re-layouts: 6.05 us -> 2.96 us
    all_to_all x3 -> x1, starting transfers between devices: 35.6 us -> 10.1 us  [body(): lax.all_to_all(whole, 'far', split_axis=0, concat_axis=0, tiled=True)]
    all_to_all x0 -> x1, blocking collectives: none -> 21.2 us  [body(): lax.all_to_all(state, 'near', split_axis=0, concat_axis=0, tiled=True)]
    pallas_call x0 -> x6, Pallas kernels: none -> 18.6 us  [the longest x1 4.78 us: body(): call(prepare_kernel, (wide, wide, wide, wide, wide, array(F32, tiles, 2 *...]
    dot_general x18 -> x0, matrix products: 14.4 us -> none  [matmul_hp(): return jnp.einsum(form, left, right, precision=lax.Precision.HIGHEST)]
    all_to_all x3 -> x1, waiting for transfers between devices: 20.8 us -> 7.75 us  [body(): lax.all_to_all(whole, 'far', split_axis=0, concat_axis=0, tiled=True)]
    conv_general_dilated x1 -> x0, matrix products: 5.84 us -> none  [causal_filter(): lax.conv_general_dilated(signal[None], kernel, (1,), 'VALID', dimension_n...]
    broadcast_in_dim x2 -> x0, local copies, waits for them, and re-layouts: 1.44 us -> none  [the longest x1 0.88 us: causal_filter(): kernel = fir_kernel[:, ::-1][:, None, :]]
    mul x2 -> x0, other arithmetic: 1.28 us -> none  [long_convolution(): -mode_dec[:, mode_index, None] * time_axis[None, :]]
  transfers between devices with their start and end apart: 4 -> 2, of which waited for: 3 -> 1; matrix products, arithmetic and copies ran while one was open for 22% -> 3% of each run, Pallas kernels for 0% -> 13%
where the time goes in v1:
time: 63.6 us; the launch traced here: 63.1 us
  blocking collectives  21.2 us (33%)
  Pallas kernels  18.6 us (29%)
  starting transfers between devices  11.9 us (19%)
  waiting for transfers between devices  7.75 us (12%)
  local copies, waits for them, and re-layouts  2.96 us (5%)
  between operations  0.67 us (1%)
    all_to_all x1, blocking collectives, body(): lax.all_to_all(state, 'near', split_axis=0, concat_axis=0, tiled=True)  21.2 us
    all_to_all x1, starting transfers between devices, body(): lax.all_to_all(whole, 'far', split_axis=0, concat_axis=0, tiled=True)  10.1 us
    all_to_all x1, waiting for transfers between devices, body(): lax.all_to_all(whole, 'far', split_axis=0, concat_axis=0, tiled=True)  7.75 us
    pallas_call x1, Pallas kernels, body(): call(prepare_kernel, (wide, wide, wide, wide, wide, array(F32, tiles, 2 *...  4.78 us
    pallas_call x1, Pallas kernels, body(): call(mix_kernel, (wide, wide, array(BF16, NEAR, tiles * modes, LANES)), (...  4.57 us
    pallas_call x1, Pallas kernels, body(): call(local_kernel, (wide, array(BF16, channels, length)), (padded,))  3.5 us
    unnamed x10, local copies, waits for them, and re-layouts  2.96 us
    pallas_call x1, Pallas kernels, body(): call(finish_kernel, array(BF16, channels, length))  2.36 us
  transfers between devices with their start and end apart: 2, of which 1 were waited for; matrix products, arithmetic and copies ran while one was open for 3% of the time, Pallas kernels for 13%

profile of v1, /device:TPU:112, one launch (start us, length us, event | category | flops | bytes accessed | tf_op | source)
XLA Modules:
  0.0 63.1 jit_solution(3962871097400186801)
XLA Ops:
  0.6 0.0 copy-start.2
  0.6 1.7 %shard_map.104.product_ref = bf16[4,128,128]{2,1,0:T(8,128)(2,1)} custom-call(bf16[512,128]{1,0:T(8,128)(2,1)} %k_ref.2, bf16[512,128]{1,0:T(8,128)(2,1)} %v_ref.1), custom_call_target="tpu_custom_call" | custom-call | tf_op jit(solution)/shard_map/pallas_call | solution.py:228
  2.4 0.0 copy-start.3
  2.4 1.9 %collective-permute-start = (bf16[4,128,128]{2,1,0:T(8,128)(2,1)}, bf16[4,128,128]{2,1,0:T(8,128)(2,1)S(1)}, u32[]{:S(2)}, u32[]{:S(2)}) collective-permute-start(bf16[4,128,128]{2,1,0:T(8,128)(2,1)} %shard_map.104.product_ref), channel_id=1, source_target_pairs={{0,16},{16,32},{32,48},{48,64},{64,80},{80,96},{96,112},{112,128},... | collective-permute-start | bytes 393224 | tf_op jit(solution)/shard_map/ppermute | solution.py:229
  4.3 0.0 copy-done.2
  4.3 0.8 %copy.11.res_ref = f32[512,16]{1,0:T(8,128)} copy(f32[512,16]{0,1:T(8,128)S(1)} %copy-done.2) | data formatting | bytes 65536 | tf_op args[6]
  5.1 0.0 copy-done.3
  5.1 0.8 %copy.12.dec_ref = f32[512,16]{1,0:T(8,128)} copy(f32[512,16]{0,1:T(8,128)S(1)} %copy-done.3) | data formatting | bytes 65536 | tf_op args[7]
  5.9 4.8 %shard_map.105 = (f32[4,128,128]{2,1,0:T(8,128)}, f32[4,128,128]{2,1,0:T(8,128)}, f32[4,128,128]{2,1,0:T(8,128)}, f32[4,128,128]{2,1,0:T(8,128)}, f32[4,128,128]{2,1,0:T(8,128)}, /*index=5*/f32[4,32,128]{2,1,0:T(8,128)}) custom-call(bf16[4,128,128]{2,1,0:T(8,128)(2,1)} %shard_map.104.product_ref, bf16[512,128]{1,0:T(8,128)(2,1)} %taps_ref.1, ...), custom_call_target="tpu_custom_call" | custom-call | tf_op jit(solution)/shard_map/pallas_call | solution.py:232
  10.7 0.0 collective-permute-done.halo_ref
  10.7 0.0 copy-start.1
  10.7 0.6 %copy-done.1 = bf16[4,128,128]{2,1,0:T(8,128)(2,1)} copy-done((bf16[4,128,128]{2,1,0:T(8,128)(2,1)}, bf16[4,128,128]{2,1,0:T(8,128)(2,1)S(1)}, u32[]{:S(2)}) %copy-start.1) | copy-done | bytes 131096
  11.4 4.6 %shard_map.106 = (f32[4,128,128]{2,1,0:T(8,128)}, f32[4,128,128]{2,1,0:T(8,128)}, bf16[8,64,128]{2,1,0:T(8,128)(2,1)}) custom-call(bf16[4,128,128]{2,1,0:T(8,128)(2,1)} %copy-done.1, f32[4,128,128]{2,1,0:T(8,128)} %get-tuple-element.15.part_ref, f32[4,128,128]{2,1,0:T(8,128)} %get-tuple-element.16.taps_ref, f32[4,128,128]{2,1,0:T(8,128)} %get-tuple-element.17.q_ref, ...), custom_call_target="tpu_custom_call" | custom-call | tf_op jit(solution)/shard_map/pallas_call | solution.py:237
  15.9 21.2 %all_to_all.10.heard_ref = bf16[8,64,128]{2,1,0:T(8,128)(2,1)} all-to-all(bf16[8,64,128]{2,1,0:T(8,128)(2,1)} %get-tuple-element.24), channel_id=1, replica_groups=mesh['far'=8,'near'=8,'chan'=16] {'near'}, dimensions={0} | all-to-all | bytes 262144 | tf_op jit(solution)/shard_map/all_to_all | solution.py:242
  37.2 1.6 %shard_map.108 = (f32[64,128]{1,0:T(8,128)}, bf16[8,64,128]{2,1,0:T(8,128)(2,1)}) custom-call(bf16[8,64,128]{2,1,0:T(8,128)(2,1)} %all_to_all.10.heard_ref, f32[4,32,128]{2,1,0:T(8,128)} %get-tuple-element.19.mode_ref), custom_call_target="tpu_custom_call" | custom-call | tf_op jit(solution)/shard_map/pallas_call | solution.py:246
  38.8 10.1 %all-to-all-start.1 = ((bf16[8,64,128]{2,1,0:T(8,128)(2,1)}), bf16[8,64,128]{2,1,0:T(8,128)(2,1)S(1)}, u32[]{:S(2)}, u32[]{:S(2)}) async-start(bf16[8,64,128]{2,1,0:T(8,128)(2,1)} %get-tuple-element.25), calls=%async_computation.1 | async-start | bytes 262144 | tf_op jit(solution)/shard_map/all_to_all | solution.py:250
  48.9 3.5 %shard_map.107 = (f32[4,128,128]{2,1,0:T(8,128)}, bf16[512,128]{1,0:T(8,128)(2,1)}) custom-call(f32[4,128,128]{2,1,0:T(8,128)} %get-tuple-element.20.mixed_ref, f32[4,128,128]{2,1,0:T(8,128)} %get-tuple-element.21.filter_ref, f32[4,128,128]{2,1,0:T(8,128)} %get-tuple-element.22.one_ref), custom_call_target="tpu_custom_call" | custom-call | tf_op jit(solution)/shard_map/pallas_call | solution.py:243
  52.4 7.8 %all-to-all-done.1.heard_ref = bf16[8,64,128]{2,1,0:T(8,128)(2,1)S(1)} async-done(((bf16[8,64,128]{2,1,0:T(8,128)(2,1)}), bf16[8,64,128]{2,1,0:T(8,128)(2,1)S(1)}, u32[]{:S(2)}, u32[]{:S(2)}) %all-to-all-start.1) | async-done | bytes 131104 | tf_op jit(solution)/shard_map/all_to_all | solution.py:250
  60.1 0.0 copy-start
  60.1 0.6 %copy-done = bf16[8,64,128]{2,1,0:T(8,128)(2,1)} copy-done((bf16[8,64,128]{2,1,0:T(8,128)(2,1)}, bf16[8,64,128]{2,1,0:T(8,128)(2,1)S(1)}, u32[]{:S(2)}) %copy-start) | copy-done | bytes 131096
  60.8 2.4 %shard_map.109 = bf16[512,128]{1,0:T(8,128)(2,1)} custom-call(bf16[8,64,128]{2,1,0:T(8,128)(2,1)} %copy-done, f32[64,128]{1,0:T(8,128)} %get-tuple-element.26.before_ref, f32[4,32,128]{2,1,0:T(8,128)} %get-tuple-element.19.mode_ref, f32[4,128,128]{2,1,0:T(8,128)} %get-tuple-element.27.conv_ref, f32[4,128,128]{2,1,0:T(8,128)} %get-tuple-element.20.mixed_ref, ...), custom_call_target="tpu_custom_call" | custom-call | tf_op jit(solution)/shard_map/pallas_call | solution.py:251
Async XLA Ops:
  0.6 3.6 %copy-start.2 = (f32[512,16]{0,1:T(8,128)S(1)}, f32[512,16]{0,1:T(8,128)}, u32[]{:S(2)}) copy-start(f32[512,16]{0,1:T(8,128)} %param.15) | copy-start | bytes 98308
  2.4 2.7 %copy-start.3 = (f32[512,16]{0,1:T(8,128)S(1)}, f32[512,16]{0,1:T(8,128)}, u32[]{:S(2)}) copy-start(f32[512,16]{0,1:T(8,128)} %param.16) | copy-start | bytes 98308
  2.4 8.3 %collective-permute-start = (bf16[4,128,128]{2,1,0:T(8,128)(2,1)}, bf16[4,128,128]{2,1,0:T(8,128)(2,1)S(1)}, u32[]{:S(2)}, u32[]{:S(2)}) collective-permute-start(bf16[4,128,128]{2,1,0:T(8,128)(2,1)} %shard_map.104.product_ref), channel_id=1, source_target_pairs={{0,16},{16,32},{32,48},{48,64},{64,80},{80,96},{96,112},{112,128},... | collective-permute-start | bytes 393224 | tf_op jit(solution)/shard_map/ppermute | solution.py:229
  10.7 0.7 %copy-start.1 = (bf16[4,128,128]{2,1,0:T(8,128)(2,1)}, bf16[4,128,128]{2,1,0:T(8,128)(2,1)S(1)}, u32[]{:S(2)}) copy-start(bf16[4,128,128]{2,1,0:T(8,128)(2,1)S(1)} %collective-permute-done.halo_ref) | copy-start | bytes 393220
  38.8 21.3 %all-to-all-start.1 = ((bf16[8,64,128]{2,1,0:T(8,128)(2,1)}), bf16[8,64,128]{2,1,0:T(8,128)(2,1)S(1)}, u32[]{:S(2)}, u32[]{:S(2)}) async-start(bf16[8,64,128]{2,1,0:T(8,128)(2,1)} %get-tuple-element.25), calls=%async_computation.1 | async-start | bytes 262144 | tf_op jit(solution)/shard_map/all_to_all | solution.py:250
  60.1 0.6 %copy-start = (bf16[8,64,128]{2,1,0:T(8,128)(2,1)}, bf16[8,64,128]{2,1,0:T(8,128)(2,1)S(1)}, u32[]{:S(2)}) copy-start(bf16[8,64,128]{2,1,0:T(8,128)(2,1)S(1)} %all-to-all-done.1.heard_ref) | copy-start | bytes 393220

commit v2 on v1

v2 whole, which is shorter than its diff:
```python
import jax
import jax.numpy as jnp
from jax import lax
from jax.experimental import pallas as pl
from jax.experimental.pallas import tpu as pltpu
from jax.sharding import Mesh, PartitionSpec as P

LANES = 128
ROWS = 8
F32 = jnp.float32
BF16 = jnp.bfloat16
LINE = 4
CORES = 2


def call(kernel, outs, scratch=()):
    return pl.pallas_call(kernel, out_shape=outs, scratch_shapes=list(scratch))


def near_by(*args):
    return [pltpu.with_memory_space_constraint(arg, pltpu.VMEM) for arg in args]


def array(dtype, *shape):
    return pltpu.VMEM(shape, dtype)


def turned(block):
    return jnp.swapaxes(block.astype(F32), 0, 1)


def rows_of(ref, tile, first, count=ROWS):
    return ref[tile, pl.ds(first, count), :]


def spread(ref, tile, row):
    return jnp.broadcast_to(ref[tile, pl.ds(row, 1), :], (ROWS, LANES))


def product_kernel(k_ref, v_ref, res_ref, dec_ref, gain_ref, out_ref, mode_out):
    modes = res_ref.shape[0]
    for tile in range(out_ref.shape[0]):
        part = pl.ds(tile * LANES, LANES)
        product = (k_ref[part, :].astype(F32) * v_ref[part, :].astype(F32)).astype(BF16)
        out_ref[tile] = turned(product).astype(BF16)
        mode_out[tile, pl.ds(0, modes), :] = res_ref[:, part]
        mode_out[tile, pl.ds(modes, modes), :] = dec_ref[:, part]
        mode_out[tile, pl.ds(2 * modes, 1), :] = gain_ref[pl.ds(tile, 1), :]


def own_taps(signal_ref, taps_ref, tile, blocks):
    sums = [jnp.zeros((ROWS, LANES), F32) for _ in range(blocks)]
    for offset in range(ROWS):
        shifted = [rows_of(signal_ref, tile, ROWS + ROWS * at - offset) for at in range(blocks)]
        for step in range(blocks):
            weight = spread(taps_ref, tile, ROWS * step + offset)
            for at in range(step, blocks):
                sums[at] = sums[at] + weight * shifted[at - step]
    return sums


def earlier_taps(sums, signal_ref, taps_ref, tile, blocks):
    sums = list(sums)
    for offset in range(ROWS):
        shifted = {
            at: rows_of(signal_ref, tile, ROWS * (blocks + at) - offset)
            for at in range(1 - blocks, 1 if offset else 0)
        }
        for step in range(blocks):
            weight = spread(taps_ref, tile, ROWS * step + offset)
            for at in range(blocks):
                if at - step in shifted:
                    sums[at] = sums[at] + weight * shifted[at - step]
    return sums


def decayed_sums(starts, decay, blocks):
    out = []
    for at in range(blocks):
        terms = list(starts)
        while len(terms) > 1:
            terms = [a + b for a, b in zip(terms[::2], terms[1::2])]
        out.append(terms[0])
        if at + 1 < blocks:
            starts = [a * b for a, b in zip(starts, decay)]
    return out


def own_filter_kernel(product_ref, taps_ref, taps_out, part_out, signal_ref):
    tiles, length = product_ref.shape[0], product_ref.shape[1]
    blocks = length // ROWS
    signal_ref[:, pl.ds(0, ROWS), :] = jnp.zeros((tiles, ROWS, LANES), F32)
    for tile in range(tiles):
        signal_ref[tile, pl.ds(ROWS, length), :] = product_ref[tile].astype(F32)
        taps_out[tile] = turned(taps_ref[pl.ds(tile * LANES, LANES), :])

    def one_tile(tile, carry):
        sums = own_taps(signal_ref, taps_out, tile, blocks)
        for at in range(blocks):
            part_out[tile, pl.ds(ROWS * at, ROWS), :] = sums[at]
        return carry

    lax.fori_loop(0, tiles, one_tile, 0)


def turn_kernel(q_ref, k_ref, q_out, k_out):
    for tile in range(q_out.shape[0]):
        part = pl.ds(tile * LANES, LANES)
        q_out[tile] = turned(q_ref[part, :])
        k_out[tile] = turned(k_ref[part, :])


def mix_kernel(
    halo_ref, part_ref, taps_ref, q_ref, k_ref, mode_ref,
    one_out, mixed_out, state_out,
    signal_ref,
):
    tiles, length = part_ref.shape[0], part_ref.shape[1]
    blocks = length // ROWS
    modes = state_out.shape[1] // tiles
    signal_ref[:, pl.ds(length, ROWS), :] = jnp.zeros((tiles, ROWS, LANES), F32)
    for tile in range(tiles):
        signal_ref[tile, pl.ds(0, length), :] = halo_ref[tile].astype(F32)

    left = (ROWS - 1 - lax.broadcasted_iota(jnp.int32, (ROWS, LANES), 0)).astype(F32)

    def one_tile(tile, carry):
        sums = [rows_of(part_ref, tile, ROWS * at) for at in range(blocks)]
        sums = earlier_taps(sums, signal_ref, taps_ref, tile, blocks)
        mixed = []
        for at in range(blocks):
            rows = pl.ds(ROWS * at, ROWS)
            first = (q_ref[tile, rows, :] * sums[at]).astype(BF16).astype(F32)
            mixed.append((k_ref[tile, rows, :] * first).astype(BF16).astype(F32))
            one_out[tile, rows, :] = first
            mixed_out[tile, rows, :] = mixed[-1]
        found = []
        for mode in range(modes):
            rate = spread(mode_ref, tile, modes + mode)
            decay = jnp.exp(-rate * float(ROWS))
            held = mixed[0]
            for at in range(1, blocks):
                held = held * decay + mixed[at]
            found.append(jnp.sum(held * jnp.exp(-rate * left), axis=0, keepdims=True))
        state = jnp.concatenate(found, axis=0).astype(BF16)
        for peer in range(state_out.shape[0]):
            state_out[peer, pl.ds(pl.multiple_of(tile * modes, modes), modes), :] = state
        return carry

    lax.fori_loop(0, tiles, one_tile, 0)


def local_conv(first, count, mixed_ref, mode_ref, conv_out, signal_ref, filter_ref):
    length = mixed_ref.shape[1]
    blocks = length // ROWS
    modes = (mode_ref.shape[1] - ROWS) // 2
    place = lax.broadcasted_iota(jnp.int32, (ROWS, LANES), 0).astype(F32)
    signal_ref[:, pl.ds(0, ROWS), :] = jnp.zeros((count, ROWS, LANES), F32)
    for tile in range(count):
        signal_ref[tile, pl.ds(ROWS, length), :] = mixed_ref[first + tile]

    def one_tile(tile, carry):
        starts, decay = [], []
        for mode in range(modes):
            rate = spread(mode_ref, first + tile, modes + mode)
            starts.append(spread(mode_ref, first + tile, mode) * jnp.exp(-rate * place))
            decay.append(jnp.exp(-rate * float(ROWS)))
        for at, value in enumerate(decayed_sums(starts, decay, blocks)):
            filter_ref[tile, pl.ds(ROWS * at, ROWS), :] = value
        sums = own_taps(signal_ref, filter_ref, tile, blocks)
        for at in range(blocks):
            conv_out[tile, pl.ds(ROWS * at, ROWS), :] = sums[at]
        return carry

    lax.fori_loop(0, count, one_tile, 0)


def first_local_kernel(mixed_ref, mode_ref, conv_out, signal_ref, filter_ref):
    local_conv(0, conv_out.shape[0], mixed_ref, mode_ref, conv_out, signal_ref, filter_ref)


def last_local_kernel(mixed_ref, mode_ref, one_ref, before_ref, conv_out, one_out, signal_ref, filter_ref):
    del before_ref
    count = conv_out.shape[0]
    local_conv(mixed_ref.shape[0] - count, count, mixed_ref, mode_ref, conv_out, signal_ref, filter_ref)
    for tile in range(one_ref.shape[0]):
        one_out[pl.ds(tile * LANES, LANES), :] = turned(one_ref[tile]).astype(BF16)


def near_kernel(heard_ref, mode_ref, conv_ref, before_out, whole_out):
    del conv_ref
    tiles, modes = mode_ref.shape[0], (mode_ref.shape[1] - ROWS) // 2
    chips = whole_out.shape[0]
    line, ring, core = lax.axis_index("line"), lax.axis_index("ring"), lax.axis_index("core")
    cores = lax.axis_size("core")
    ahead = (core * LANES).astype(F32)
    for tile in range(tiles):
        part = pl.ds(tile * modes, modes)
        rates = mode_ref[tile, pl.ds(modes, modes), :]
        step = jnp.exp(-rates * float(LANES))
        row = jnp.exp(-rates * float(LANES * cores * chips))
        lead = jnp.exp(-rates * ahead)
        zero = jnp.zeros((modes, LANES), F32)
        whole, earlier, upto, before = zero, zero, zero, zero
        for other in range(heard_ref.shape[0] // cores):
            chip = zero
            for peer in range(cores):
                chip = chip * step + heard_ref[other * cores + peer, part, :].astype(F32)
                before = jnp.where((other == line) & (peer < core), chip, before)
            whole = whole * row + chip * lead
            earlier = jnp.where(other < line, whole, earlier)
            upto = jnp.where(other == line, whole, upto)
        before_out[part, :] = before
        for peer in range(chips):
            whole_out[peer, part, :] = jnp.where(peer > ring, upto, earlier).astype(BF16)


def finish_kernel(heard_ref, before_ref, mode_ref, early_ref, late_ref, mixed_ref, gate_ref, out_ref):
    tiles, length = mixed_ref.shape[0], mixed_ref.shape[1]
    blocks = length // ROWS
    modes = (mode_ref.shape[1] - ROWS) // 2
    chips = heard_ref.shape[0]
    ring = lax.axis_index("ring")
    order = [lax.rem(ring + at, chips) for at in range(chips)]
    after = (1 + lax.broadcasted_iota(jnp.int32, (ROWS, LANES), 0)).astype(F32)
    for tile in range(tiles):
        part = pl.ds(tile * modes, modes)
        rates = mode_ref[tile, pl.ds(modes, modes), :]
        step = jnp.exp(-rates * float(length * lax.axis_size("core")))
        far = heard_ref[order[0], part, :].astype(F32)
        for peer in order[1:]:
            far = far * step + heard_ref[peer, part, :].astype(F32)
        entering = (before_ref[part, :] + far) * mode_ref[tile, pl.ds(0, modes), :]
        starts, decay = [], []
        for mode in range(modes):
            rate = jnp.broadcast_to(rates[mode : mode + 1, :], (ROWS, LANES))
            starts.append(jnp.broadcast_to(entering[mode : mode + 1, :], (ROWS, LANES)) * jnp.exp(-rate * after))
            decay.append(jnp.exp(-rate * float(ROWS)))
        gain = spread(mode_ref, tile, 2 * modes)
        early = early_ref.shape[0]
        conv_ref, at_tile = (early_ref, tile) if tile < early else (late_ref, tile - early)
        made = []
        for at, value in enumerate(decayed_sums(starts, decay, blocks)):
            rows = pl.ds(ROWS * at, ROWS)
            convolved = (conv_ref[at_tile, rows, :] + value).astype(BF16).astype(F32)
            made.append(convolved + gain * mixed_ref[tile, rows, :])
        channels = pl.ds(tile * LANES, LANES)
        summed = turned(jnp.concatenate(made, axis=0))
        out_ref[channels, :] = (gate_ref[channels, :].astype(F32) * summed).astype(BF16)


def body(q_one, k_one, v_one, fir_taps, q_two, k_two, residues, decays, skip_gain):
    channels, length = q_one.shape
    tiles, modes = channels // LANES, residues.shape[1]
    seq = ("line", "ring", "core")
    chips = lax.axis_size("ring")
    mates = lax.axis_size("line") * lax.axis_size("core")
    count = mates * chips
    wide = array(F32, tiles, length, LANES)
    states = tiles * modes
    product, mode_rows = call(
        product_kernel,
        (array(BF16, tiles, length, LANES), array(F32, tiles, 2 * modes + ROWS, LANES)),
    )(k_one, v_one, residues.T, decays.T, skip_gain.reshape(tiles, LANES))
    halo = lax.ppermute(product, seq, [(at, at + 1) for at in range(count - 1)])
    padded = pltpu.VMEM((tiles, length + ROWS, LANES), F32)
    taps, part = call(own_filter_kernel, (wide, wide), (padded,))(*near_by(product, fir_taps))
    q_turned, k_turned = call(turn_kernel, (wide, wide))(*near_by(q_one, k_two))
    one_turned, mixed, state = call(
        mix_kernel, (wide, wide, array(BF16, mates, states, LANES)), (padded,)
    )(*near_by(halo, part, taps, q_turned, k_turned, mode_rows))
    heard = lax.all_to_all(state, ("line", "core"), split_axis=0, concat_axis=0, tiled=True)
    early = tiles // 2
    held = array(F32, early, length, LANES)
    scratch = (pltpu.VMEM((early, length + ROWS, LANES), F32), pltpu.VMEM((early, length, LANES), F32))
    early_conv = call(first_local_kernel, held, scratch)(*near_by(mixed, mode_rows))
    before, whole = call(
        near_kernel, (array(F32, states, LANES), array(BF16, chips, states, LANES))
    )(*near_by(heard, mode_rows, early_conv))
    far_heard = lax.all_to_all(whole, "ring", split_axis=0, concat_axis=0, tiled=True)
    late_conv, layer_one = call(
        last_local_kernel, (held, jax.ShapeDtypeStruct((channels, length), BF16)), scratch
    )(*near_by(mixed, mode_rows, one_turned, before))
    layer_two = call(finish_kernel, jax.ShapeDtypeStruct((channels, length), BF16))(
        *near_by(far_heard, before, mode_rows, early_conv, late_conv, mixed, q_two)
    )
    return (layer_one, layer_two)


def solution(mesh):
    count, chans = mesh.shape["seq"], mesh.shape["chan"]
    split = (LINE, count // (LINE * CORES), CORES)
    grid = Mesh(mesh.devices.reshape(*split, chans), ("line", "ring", "core", "chan"))
    split = P("chan", ("line", "ring", "core"))
    whole = P("chan", None)
    return jax.shard_map(
        body,
        mesh=grid,
        in_specs=(split, split, split, whole, split, split, whole, whole, P("chan")),
        out_specs=(split, split),
        check_vma=False,
    )
```

time: 63.6 us -> 50.9 us (0.80)
  blocking collectives: 21.2 us -> 0 us
  starting transfers between devices: 11.9 us -> 25.8 us
  Pallas kernels: 18.6 us -> 10.3 us
  waiting for transfers between devices: 7.75 us -> 13.6 us
  local copies, waits for them, and re-layouts: 2.96 us -> 0.02 us
    all_to_all x1 -> x0, blocking collectives: 21.2 us -> none  [body(): lax.all_to_all(state, 'near', split_axis=0, concat_axis=0, tiled=True)]
    all_to_all x1 -> x2, starting transfers between devices: 10.1 us -> 24 us  [the longest x1 20.4 us: body(): lax.all_to_all(state, ('line', 'core'), split_axis=0, concat_axis=0, tile...]
    pallas_call x6 -> x8, Pallas kernels: 18.6 us -> 10.3 us  [the longest x1 3.24 us: body(): call(mix_kernel, (wide, wide, array(BF16, mates, states, LANES)), (padded,))]
    all_to_all x1 -> x2, waiting for transfers between devices: 7.75 us -> 13.6 us  [the longest x1 7.57 us: body(): lax.all_to_all(whole, 'ring', split_axis=0, concat_axis=0, tiled=True)]
    unnamed x10 -> x8, local copies, waits for them, and re-layouts: 2.96 us -> 0.02 us
  transfers between devices with their start and end apart: 2 -> 3, of which waited for: 1 -> 2; matrix products, arithmetic and copies ran while one was open for 3% -> 0% of each run, Pallas kernels for 13% -> 8%
where the time goes in v2:
time: 50.9 us; the launch traced here: 50.5 us
  starting transfers between devices  25.8 us (51%)
  waiting for transfers between devices  13.6 us (27%)
  Pallas kernels  10.3 us (20%)
  between operations  0.73 us (1%)
    all_to_all x1, starting transfers between devices, body(): lax.all_to_all(state, ('line', 'core'), split_axis=0, concat_axis=0, tile...  20.4 us
    all_to_all x1, waiting for transfers between devices, body(): lax.all_to_all(whole, 'ring', split_axis=0, concat_axis=0, tiled=True)  7.57 us
    all_to_all x1, waiting for transfers between devices, body(): lax.all_to_all(state, ('line', 'core'), split_axis=0, concat_axis=0, tile...  5.99 us
    all_to_all x1, starting transfers between devices, body(): lax.all_to_all(whole, 'ring', split_axis=0, concat_axis=0, tiled=True)  3.6 us
    pallas_call x1, Pallas kernels, body(): call(mix_kernel, (wide, wide, array(BF16, mates, states, LANES)), (padded,))  3.24 us
    ppermute x1, starting transfers between devices, body(): halo = lax.ppermute(product, seq, [(at, at + 1) for at in range(count - 1)])  1.88 us
    pallas_call x1, Pallas kernels, body(): call(own_filter_kernel, (wide, wide), (padded,))  1.67 us
    pallas_call x1, Pallas kernels, body(): call(last_local_kernel, (held, jax.ShapeDtypeStruct((channels, length), B...  1.51 us
  transfers between devices with their start and end apart: 3, of which 2 were waited for; matrix products, arithmetic and copies ran while one was open for 0% of the time, Pallas kernels for 8%

profile of v2, /device:TPU:112, one launch (start us, length us, event | category | flops | bytes accessed | tf_op | source)
XLA Modules:
  0.0 50.5 jit_solution(11622754225120431391)
XLA Ops:
  0.6 0.0 copy-start
  0.6 1.1 %shard_map.104 = (bf16[4,128,128]{2,1,0:T(8,128)(2,1)S(1)}, f32[4,40,128]{2,1,0:T(8,128)S(1)}) custom-call(bf16[512,128]{1,0:T(8,128)(2,1)} %k_ref.2, bf16[512,128]{1,0:T(8,128)(2,1)} %v_ref.1, f32[16,512]{1,0:T(8,128)} %bitcast.3, f32[16,512]{1,0:T(8,128)} %bitcast.4, f32[4,128]{1,0:T(4,128)} %bitcast.5), custom_call_target="tpu_custom_call" | custom-call | tf_op jit(solution)/shard_map/pallas_call | solution.py:261
  1.8 0.0 copy-start.1
  1.8 0.0 copy-start.2
  1.8 1.9 %collective-permute-start = (bf16[4,128,128]{2,1,0:T(8,128)(2,1)S(1)}, bf16[4,128,128]{2,1,0:T(8,128)(2,1)S(1)}, u32[]{:S(2)}, u32[]{:S(2)}) collective-permute-start(bf16[4,128,128]{2,1,0:T(8,128)(2,1)S(1)} %get-tuple-element.15.product_ref), channel_id=1, source_target_pairs={{0,16},{16,32},{32,48},{48,64},{64,80},{80,96},{96,112},{112,128},... | collective-permute-start | bytes 393224 | tf_op jit(solution)/shard_map/ppermute | solution.py:265
  3.7 0.0 copy-done
  3.7 1.7 %shard_map.105 = (f32[4,128,128]{2,1,0:T(8,128)S(1)}, f32[4,128,128]{2,1,0:T(8,128)S(1)}) custom-call(bf16[4,128,128]{2,1,0:T(8,128)(2,1)S(1)} %get-tuple-element.15.product_ref, bf16[512,128]{1,0:T(8,128)(2,1)S(1)} %copy-done), custom_call_target="tpu_custom_call" | custom-call | tf_op jit(solution)/shard_map/pallas_call | solution.py:267
  5.4 0.0 copy-done.1
  5.4 0.0 copy-done.2
  5.4 0.1 shard_map.106
  5.5 0.0 collective-permute-done.halo_ref
  5.6 3.2 %shard_map.107 = (f32[4,128,128]{2,1,0:T(8,128)S(1)}, f32[4,128,128]{2,1,0:T(8,128)S(1)}, bf16[8,64,128]{2,1,0:T(8,128)(2,1)}) custom-call(bf16[4,128,128]{2,1,0:T(8,128)(2,1)S(1)} %collective-permute-done.halo_ref, f32[4,128,128]{2,1,0:T(8,128)S(1)} %get-tuple-element.16.part_ref, f32[4,128,128]{2,1,0:T(8,128)S(1)} %get-tuple-element.17.taps_ref, ...), custom_call_target="tpu_custom_call" | custom-call | tf_op jit(solution)/shard_map/pallas_call | solution.py:269
  8.8 20.4 %all-to-all-start = ((bf16[8,64,128]{2,1,0:T(8,128)(2,1)}), bf16[8,64,128]{2,1,0:T(8,128)(2,1)S(1)}, u32[]{:S(2)}, u32[]{:S(2)}) async-start(bf16[8,64,128]{2,1,0:T(8,128)(2,1)} %get-tuple-element.23), calls=%async_computation | async-start | bytes 262144 | tf_op jit(solution)/shard_map/all_to_all | solution.py:272
  29.2 0.7 %shard_map.108.conv_ref.early_ref = f32[2,128,128]{2,1,0:T(8,128)S(1)} custom-call(f32[4,128,128]{2,1,0:T(8,128)S(1)} %get-tuple-element.21.mixed_ref, f32[4,40,128]{2,1,0:T(8,128)S(1)} %get-tuple-element.20.mode_ref), custom_call_target="tpu_custom_call" | custom-call | tf_op jit(solution)/shard_map/pallas_call | solution.py:276
  29.9 6.0 %all-to-all-done.heard_ref = bf16[8,64,128]{2,1,0:T(8,128)(2,1)S(1)} async-done(((bf16[8,64,128]{2,1,0:T(8,128)(2,1)}), bf16[8,64,128]{2,1,0:T(8,128)(2,1)S(1)}, u32[]{:S(2)}, u32[]{:S(2)}) %all-to-all-start) | async-done | bytes 131104 | tf_op jit(solution)/shard_map/all_to_all | solution.py:272
  35.9 0.7 %shard_map.109 = (f32[64,128]{1,0:T(8,128)S(1)}, bf16[8,64,128]{2,1,0:T(8,128)(2,1)}) custom-call(bf16[8,64,128]{2,1,0:T(8,128)(2,1)S(1)} %all-to-all-done.heard_ref, f32[4,40,128]{2,1,0:T(8,128)S(1)} %get-tuple-element.20.mode_ref, f32[2,128,128]{2,1,0:T(8,128)S(1)} %shard_map.108.conv_ref.early_ref), custom_call_target="tpu_custom_call" | custom-call | tf_op jit(solution)/shard_map/pallas_call | solution.py:277
  36.6 3.6 %all-to-all-start.1 = ((bf16[8,64,128]{2,1,0:T(8,128)(2,1)}), bf16[8,64,128]{2,1,0:T(8,128)(2,1)S(1)}, u32[]{:S(2)}, u32[]{:S(2)}) async-start(bf16[8,64,128]{2,1,0:T(8,128)(2,1)} %get-tuple-element.26), calls=%async_computation.1 | async-start | bytes 262144 | tf_op jit(solution)/shard_map/all_to_all | solution.py:280
  40.2 0.0 copy-start.3
  40.3 1.5 %shard_map.110 = (f32[2,128,128]{2,1,0:T(8,128)S(1)}, bf16[512,128]{1,0:T(8,128)(2,1)}) custom-call(f32[4,128,128]{2,1,0:T(8,128)S(1)} %get-tuple-element.21.mixed_ref, f32[4,40,128]{2,1,0:T(8,128)S(1)} %get-tuple-element.20.mode_ref, f32[4,128,128]{2,1,0:T(8,128)S(1)} %get-tuple-element.22.one_ref, f32[64,128]{1,0:T(8,128)S(1)} %get-tuple-element.24.before_ref), custom_call_target="tpu_custom_call" | custom-call | tf_op jit(solution)/shard_map/pallas_call | solution.py:281
  41.8 7.6 %all-to-all-done.1.heard_ref = bf16[8,64,128]{2,1,0:T(8,128)(2,1)S(1)} async-done(((bf16[8,64,128]{2,1,0:T(8,128)(2,1)}), bf16[8,64,128]{2,1,0:T(8,128)(2,1)S(1)}, u32[]{:S(2)}, u32[]{:S(2)}) %all-to-all-start.1) | async-done | bytes 131104 | tf_op jit(solution)/shard_map/all_to_all | solution.py:280
  49.3 0.0 copy-done.3
  49.3 1.2 %shard_map.111 = bf16[512,128]{1,0:T(8,128)(2,1)} custom-call(bf16[8,64,128]{2,1,0:T(8,128)(2,1)S(1)} %all-to-all-done.1.heard_ref, f32[64,128]{1,0:T(8,128)S(1)} %get-tuple-element.24.before_ref, f32[4,40,128]{2,1,0:T(8,128)S(1)} %get-tuple-element.20.mode_ref, f32[2,128,128]{2,1,0:T(8,128)S(1)} %shard_map.108.conv_ref.early_ref, ...), custom_call_target="tpu_custom_call" | custom-call | tf_op jit(solution)/shard_map/pallas_call | solution.py:284
Async XLA Ops:
  0.6 3.1 %copy-start = (bf16[512,128]{1,0:T(8,128)(2,1)S(1)}, bf16[512,128]{1,0:T(8,128)(2,1)}, u32[]{:S(2)}) copy-start(bf16[512,128]{1,0:T(8,128)(2,1)} %taps_ref.1) | copy-start | bytes 393220
  1.8 3.6 %copy-start.1 = (bf16[512,128]{1,0:T(8,128)(2,1)S(1)}, bf16[512,128]{1,0:T(8,128)(2,1)}, u32[]{:S(2)}) copy-start(bf16[512,128]{1,0:T(8,128)(2,1)} %q_ref.1) | copy-start | bytes 393220
  1.8 3.6 %copy-start.2 = (bf16[512,128]{1,0:T(8,128)(2,1)S(1)}, bf16[512,128]{1,0:T(8,128)(2,1)}, u32[]{:S(2)}) copy-start(bf16[512,128]{1,0:T(8,128)(2,1)} %k_ref.3) | copy-start | bytes 393220
  1.8 3.7 %collective-permute-start = (bf16[4,128,128]{2,1,0:T(8,128)(2,1)S(1)}, bf16[4,128,128]{2,1,0:T(8,128)(2,1)S(1)}, u32[]{:S(2)}, u32[]{:S(2)}) collective-permute-start(bf16[4,128,128]{2,1,0:T(8,128)(2,1)S(1)} %get-tuple-element.15.product_ref), channel_id=1, source_target_pairs={{0,16},{16,32},{32,48},{48,64},{64,80},{80,96},{96,112},{112,128},... | collective-permute-start | bytes 393224 | tf_op jit(solution)/shard_map/ppermute | solution.py:265
  8.8 27.1 %all-to-all-start = ((bf16[8,64,128]{2,1,0:T(8,128)(2,1)}), bf16[8,64,128]{2,1,0:T(8,128)(2,1)S(1)}, u32[]{:S(2)}, u32[]{:S(2)}) async-start(bf16[8,64,128]{2,1,0:T(8,128)(2,1)} %get-tuple-element.23), calls=%async_computation | async-start | bytes 262144 | tf_op jit(solution)/shard_map/all_to_all | solution.py:272
  36.6 12.7 %all-to-all-start.1 = ((bf16[8,64,128]{2,1,0:T(8,128)(2,1)}), bf16[8,64,128]{2,1,0:T(8,128)(2,1)S(1)}, u32[]{:S(2)}, u32[]{:S(2)}) async-start(bf16[8,64,128]{2,1,0:T(8,128)(2,1)} %get-tuple-element.26), calls=%async_computation.1 | async-start | bytes 262144 | tf_op jit(solution)/shard_map/all_to_all | solution.py:280
  40.2 9.1 %copy-start.3 = (bf16[512,128]{1,0:T(8,128)(2,1)S(1)}, bf16[512,128]{1,0:T(8,128)(2,1)}, u32[]{:S(2)}) copy-start(bf16[512,128]{1,0:T(8,128)(2,1)} %gate_ref.1) | copy-start | bytes 393220

commit v3 on v2

--- a/solution.py
+++ b/solution.py
@@ -60,18 +60,16 @@
 
 
 def earlier_taps(sums, signal_ref, taps_ref, tile, blocks):
-    sums = list(sums)
-    for offset in range(ROWS):
-        shifted = {
-            at: rows_of(signal_ref, tile, ROWS * (blocks + at) - offset)
-            for at in range(1 - blocks, 1 if offset else 0)
-        }
+    def one_offset(offset, sums):
+        sums = list(sums)
+        shifted = [rows_of(signal_ref, tile, ROWS * (blocks - at) - offset) for at in range(blocks)]
         for step in range(blocks):
             weight = spread(taps_ref, tile, ROWS * step + offset)
-            for at in range(blocks):
-                if at - step in shifted:
-                    sums[at] = sums[at] + weight * shifted[at - step]
-    return sums
+            for at in range(step + 1):
+                sums[at] = sums[at] + weight * shifted[step - at]
+        return tuple(sums)
+
+    return list(lax.fori_loop(0, ROWS, one_offset, tuple(sums)))
 
 
 def decayed_sums(starts, decay, blocks):
@@ -176,6 +174,10 @@
 
 
 def first_local_kernel(mixed_ref, mode_ref, conv_out, signal_ref, filter_ref):
+    local_conv(0, conv_out.shape[0], mixed_ref, mode_ref, conv_out, signal_ref, filter_ref)
+
+
+def early_after_kernel(mixed_ref, mode_ref, before_ref, conv_out, signal_ref, filter_ref):
     local_conv(0, conv_out.shape[0], mixed_ref, mode_ref, conv_out, signal_ref, filter_ref)
 
 
@@ -273,11 +275,11 @@
     early = tiles // 2
     held = array(F32, early, length, LANES)
     scratch = (pltpu.VMEM((early, length + ROWS, LANES), F32), pltpu.VMEM((early, length, LANES), F32))
-    early_conv = call(first_local_kernel, held, scratch)(*near_by(mixed, mode_rows))
     before, whole = call(
         near_kernel, (array(F32, states, LANES), array(BF16, chips, states, LANES))
-    )(*near_by(heard, mode_rows, early_conv))
+    )(*near_by(heard, mode_rows, mode_rows))
     far_heard = lax.all_to_all(whole, "ring", split_axis=0, concat_axis=0, tiled=True)
+    early_conv = call(early_after_kernel, held, scratch)(*near_by(mixed, mode_rows, before))
     late_conv, layer_one = call(
         last_local_kernel, (held, jax.ShapeDtypeStruct((channels, length), BF16)), scratch
     )(*near_by(mixed, mode_rows, one_turned, before))

time: 50.9 us -> 49.3 us (0.969)
  blocking collectives: 0 us -> 26.9 us
  starting transfers between devices: 25.8 us -> 5.48 us
  waiting for transfers between devices: 13.6 us -> 6.81 us
  Pallas kernels: 10.3 us -> 9.09 us
    all_to_all x0 -> x1, blocking collectives: none -> 26.9 us  [body(): lax.all_to_all(state, ('line', 'core'), split_axis=0, concat_axis=0, tile...]
    all_to_all x1 -> x0, starting transfers between devices: 20.4 us -> none  [body(): lax.all_to_all(state, ('line', 'core'), split_axis=0, concat_axis=0, tile...]
    all_to_all x1 -> x0, waiting for transfers between devices: 5.99 us -> none  [body(): lax.all_to_all(state, ('line', 'core'), split_axis=0, concat_axis=0, tile...]
    pallas_call x1, Pallas kernels: 3.24 us -> 2 us  [body(): call(mix_kernel, (wide, wide, array(BF16, mates, states, LANES)), (padded,))]
    all_to_all x1, waiting for transfers between devices: 7.57 us -> 6.81 us  [body(): lax.all_to_all(whole, 'ring', split_axis=0, concat_axis=0, tiled=True)]
  transfers between devices with their start and end apart: 3 -> 2, of which waited for: 2 -> 1; matrix products, arithmetic and copies ran while one was open for 0% -> 0% of each run, Pallas kernels for 8% -> 8%
where the time goes in v3:
time: 49.3 us; the launch traced here: 49 us
  blocking collectives  26.9 us (55%)
  Pallas kernels  9.09 us (18%)
  waiting for transfers between devices  6.81 us (14%)
  starting transfers between devices  5.48 us (11%)
  between operations  0.74 us (2%)
    all_to_all x1, blocking collectives, body(): lax.all_to_all(state, ('line', 'core'), split_axis=0, concat_axis=0, tile...  26.9 us
    all_to_all x1, waiting for transfers between devices, body(): lax.all_to_all(whole, 'ring', split_axis=0, concat_axis=0, tiled=True)  6.81 us
    all_to_all x1, starting transfers between devices, body(): lax.all_to_all(whole, 'ring', split_axis=0, concat_axis=0, tiled=True)  3.6 us
    pallas_call x1, Pallas kernels, body(): call(mix_kernel, (wide, wide, array(BF16, mates, states, LANES)), (padded,))  2 us
    ppermute x1, starting transfers between devices, body(): halo = lax.ppermute(product, seq, [(at, at + 1) for at in range(count - 1)])  1.88 us
    pallas_call x1, Pallas kernels, body(): call(own_filter_kernel, (wide, wide), (padded,))  1.67 us
    pallas_call x1, Pallas kernels, body(): call(last_local_kernel, (held, jax.ShapeDtypeStruct((channels, length), B...  1.51 us
    pallas_call x1, Pallas kernels, body(): call(finish_kernel, jax.ShapeDtypeStruct((channels, length), BF16))  1.15 us
  transfers between devices with their start and end apart: 2, of which 1 were waited for; matrix products, arithmetic and copies ran while one was open for 0% of the time, Pallas kernels for 8%

profile of v3, /device:TPU:112, one launch (start us, length us, event | category | flops | bytes accessed | tf_op | source)
XLA Modules:
  0.0 49.0 jit_solution(6499874784827792067)
XLA Ops:
  0.6 0.0 copy-start
  0.6 1.1 %shard_map.104 = (bf16[4,128,128]{2,1,0:T(8,128)(2,1)S(1)}, f32[4,40,128]{2,1,0:T(8,128)S(1)}) custom-call(bf16[512,128]{1,0:T(8,128)(2,1)} %k_ref.2, bf16[512,128]{1,0:T(8,128)(2,1)} %v_ref.1, f32[16,512]{1,0:T(8,128)} %bitcast.3, f32[16,512]{1,0:T(8,128)} %bitcast.4, f32[4,128]{1,0:T(4,128)} %bitcast.5), custom_call_target="tpu_custom_call" | custom-call | tf_op jit(solution)/shard_map/pallas_call | solution.py:263
  1.8 0.0 copy-start.1
  1.8 0.0 copy-start.2
  1.8 1.9 %collective-permute-start = (bf16[4,128,128]{2,1,0:T(8,128)(2,1)S(1)}, bf16[4,128,128]{2,1,0:T(8,128)(2,1)S(1)}, u32[]{:S(2)}, u32[]{:S(2)}) collective-permute-start(bf16[4,128,128]{2,1,0:T(8,128)(2,1)S(1)} %get-tuple-element.15.product_ref), channel_id=1, source_target_pairs={{0,16},{16,32},{32,48},{48,64},{64,80},{80,96},{96,112},{112,128},... | collective-permute-start | bytes 393224 | tf_op jit(solution)/shard_map/ppermute | solution.py:267
  3.7 0.0 copy-done
  3.7 1.7 %shard_map.105 = (f32[4,128,128]{2,1,0:T(8,128)S(1)}, f32[4,128,128]{2,1,0:T(8,128)S(1)}) custom-call(bf16[4,128,128]{2,1,0:T(8,128)(2,1)S(1)} %get-tuple-element.15.product_ref, bf16[512,128]{1,0:T(8,128)(2,1)S(1)} %copy-done), custom_call_target="tpu_custom_call" | custom-call | tf_op jit(solution)/shard_map/pallas_call | solution.py:269
  5.4 0.0 copy-done.1
  5.4 0.0 copy-done.2
  5.4 0.1 shard_map.106
  5.5 0.0 collective-permute-done.halo_ref
  5.6 2.0 %shard_map.107 = (f32[4,128,128]{2,1,0:T(8,128)S(1)}, f32[4,128,128]{2,1,0:T(8,128)S(1)}, bf16[8,64,128]{2,1,0:T(8,128)(2,1)S(1)}) custom-call(bf16[4,128,128]{2,1,0:T(8,128)(2,1)S(1)} %collective-permute-done.halo_ref, f32[4,128,128]{2,1,0:T(8,128)S(1)} %get-tuple-element.16.part_ref, f32[4,128,128]{2,1,0:T(8,128)S(1)} %get-tuple-element.17.taps_ref, ...), custom_call_target="tpu_custom_call" | custom-call | tf_op jit(solution)/shard_map/pallas_call | solution.py:271
  7.6 26.9 %all_to_all.10.heard_ref = bf16[8,64,128]{2,1,0:T(8,128)(2,1)S(1)} all-to-all(bf16[8,64,128]{2,1,0:T(8,128)(2,1)S(1)} %get-tuple-element.23), channel_id=1, replica_groups=mesh['line'=4,'ring'=8,'core'=2,'chan'=16] {'line','core'}, dimensions={0} | all-to-all | bytes 262144 | tf_op jit(solution)/shard_map/all_to_all | solution.py:274
  34.5 0.7 %shard_map.108 = (f32[64,128]{1,0:T(8,128)S(1)}, bf16[8,64,128]{2,1,0:T(8,128)(2,1)}) custom-call(bf16[8,64,128]{2,1,0:T(8,128)(2,1)S(1)} %all_to_all.10.heard_ref, f32[4,40,128]{2,1,0:T(8,128)S(1)} %get-tuple-element.20.mode_ref.conv_ref, f32[4,40,128]{2,1,0:T(8,128)S(1)} %get-tuple-element.20.mode_ref.conv_ref), custom_call_target="tpu_custom_call" | custom-call | tf_op jit(solution)/shard_map/pallas_call | solution.py:278
  35.2 3.6 %all-to-all-start.1 = ((bf16[8,64,128]{2,1,0:T(8,128)(2,1)}), bf16[8,64,128]{2,1,0:T(8,128)(2,1)S(1)}, u32[]{:S(2)}, u32[]{:S(2)}) async-start(bf16[8,64,128]{2,1,0:T(8,128)(2,1)} %get-tuple-element.26), calls=%async_computation.1 | async-start | bytes 262144 | tf_op jit(solution)/shard_map/all_to_all | solution.py:281
  38.8 0.7 %shard_map.110.early_ref = f32[2,128,128]{2,1,0:T(8,128)S(1)} custom-call(f32[4,128,128]{2,1,0:T(8,128)S(1)} %get-tuple-element.21.mixed_ref, f32[4,40,128]{2,1,0:T(8,128)S(1)} %get-tuple-element.20.mode_ref.conv_ref, f32[64,128]{1,0:T(8,128)S(1)} %get-tuple-element.24.before_ref), custom_call_target="tpu_custom_call" | custom-call | tf_op jit(solution)/shard_map/pallas_call | solution.py:282
  39.6 0.0 copy-start.3
  39.6 1.5 %shard_map.109 = (f32[2,128,128]{2,1,0:T(8,128)S(1)}, bf16[512,128]{1,0:T(8,128)(2,1)}) custom-call(f32[4,128,128]{2,1,0:T(8,128)S(1)} %get-tuple-element.21.mixed_ref, f32[4,40,128]{2,1,0:T(8,128)S(1)} %get-tuple-element.20.mode_ref.conv_ref, f32[4,128,128]{2,1,0:T(8,128)S(1)} %get-tuple-element.22.one_ref, f32[64,128]{1,0:T(8,128)S(1)} %get-tuple-element.24.before_ref), custom_call_target="tpu_custom_call" | custom-call | tf_op jit(solution)/shard_map/pallas_call | solution.py:283
  41.1 6.8 %all-to-all-done.1.heard_ref = bf16[8,64,128]{2,1,0:T(8,128)(2,1)S(1)} async-done(((bf16[8,64,128]{2,1,0:T(8,128)(2,1)}), bf16[8,64,128]{2,1,0:T(8,128)(2,1)S(1)}, u32[]{:S(2)}, u32[]{:S(2)}) %all-to-all-start.1) | async-done | bytes 131104 | tf_op jit(solution)/shard_map/all_to_all | solution.py:281
  47.9 0.0 copy-done.3
  47.9 1.2 %shard_map.111 = bf16[512,128]{1,0:T(8,128)(2,1)} custom-call(bf16[8,64,128]{2,1,0:T(8,128)(2,1)S(1)} %all-to-all-done.1.heard_ref, f32[64,128]{1,0:T(8,128)S(1)} %get-tuple-element.24.before_ref, f32[4,40,128]{2,1,0:T(8,128)S(1)} %get-tuple-element.20.mode_ref.conv_ref, f32[2,128,128]{2,1,0:T(8,128)S(1)} %shard_map.110.early_ref, ...), custom_call_target="tpu_custom_call" | custom-call | tf_op jit(solution)/shard_map/pallas_call | solution.py:286
Async XLA Ops:
  0.6 3.1 %copy-start = (bf16[512,128]{1,0:T(8,128)(2,1)S(1)}, bf16[512,128]{1,0:T(8,128)(2,1)}, u32[]{:S(2)}) copy-start(bf16[512,128]{1,0:T(8,128)(2,1)} %taps_ref.1) | copy-start | bytes 393220
  1.8 3.6 %copy-start.1 = (bf16[512,128]{1,0:T(8,128)(2,1)S(1)}, bf16[512,128]{1,0:T(8,128)(2,1)}, u32[]{:S(2)}) copy-start(bf16[512,128]{1,0:T(8,128)(2,1)} %q_ref.1) | copy-start | bytes 393220
  1.8 3.6 %copy-start.2 = (bf16[512,128]{1,0:T(8,128)(2,1)S(1)}, bf16[512,128]{1,0:T(8,128)(2,1)}, u32[]{:S(2)}) copy-start(bf16[512,128]{1,0:T(8,128)(2,1)} %k_ref.3) | copy-start | bytes 393220
  1.8 3.7 %collective-permute-start = (bf16[4,128,128]{2,1,0:T(8,128)(2,1)S(1)}, bf16[4,128,128]{2,1,0:T(8,128)(2,1)S(1)}, u32[]{:S(2)}, u32[]{:S(2)}) collective-permute-start(bf16[4,128,128]{2,1,0:T(8,128)(2,1)S(1)} %get-tuple-element.15.product_ref), channel_id=1, source_target_pairs={{0,16},{16,32},{32,48},{48,64},{64,80},{80,96},{96,112},{112,128},... | collective-permute-start | bytes 393224 | tf_op jit(solution)/shard_map/ppermute | solution.py:267
  35.2 12.7 %all-to-all-start.1 = ((bf16[8,64,128]{2,1,0:T(8,128)(2,1)}), bf16[8,64,128]{2,1,0:T(8,128)(2,1)S(1)}, u32[]{:S(2)}, u32[]{:S(2)}) async-start(bf16[8,64,128]{2,1,0:T(8,128)(2,1)} %get-tuple-element.26), calls=%async_computation.1 | async-start | bytes 262144 | tf_op jit(solution)/shard_map/all_to_all | solution.py:281
  39.6 8.3 %copy-start.3 = (bf16[512,128]{1,0:T(8,128)(2,1)S(1)}, bf16[512,128]{1,0:T(8,128)(2,1)}, u32[]{:S(2)}) copy-start(bf16[512,128]{1,0:T(8,128)(2,1)} %gate_ref.1) | copy-start | bytes 393220

commit v4 on v3

--- a/solution.py
+++ b/solution.py
@@ -1,5 +1,6 @@
 import jax
 import jax.numpy as jnp
+import numpy as np
 from jax import lax
 from jax.experimental import pallas as pl
 from jax.experimental.pallas import tpu as pltpu
@@ -14,7 +15,8 @@
 
 
 def call(kernel, outs, scratch=()):
-    return pl.pallas_call(kernel, out_shape=outs, scratch_shapes=list(scratch))
+    limit = pltpu.CompilerParams(vmem_limit_bytes=16 << 20)
+    return pl.pallas_call(kernel, out_shape=outs, scratch_shapes=list(scratch), compiler_params=limit)
 
 
 def near_by(*args):
@@ -59,17 +61,32 @@
     return sums
 
 
-def earlier_taps(sums, signal_ref, taps_ref, tile, blocks):
-    def one_offset(offset, sums):
-        sums = list(sums)
-        shifted = [rows_of(signal_ref, tile, ROWS * (blocks - at) - offset) for at in range(blocks)]
-        for step in range(blocks):
-            weight = spread(taps_ref, tile, ROWS * step + offset)
-            for at in range(step + 1):
-                sums[at] = sums[at] + weight * shifted[step - at]
-        return tuple(sums)
-
-    return list(lax.fori_loop(0, ROWS, one_offset, tuple(sums)))
+def spectrum_tables(length):
+    points = 2 * length
+    angle = 2.0 * np.pi / points * (np.arange(length)[:, None] * np.arange(points)[None, :] % points)
+    real, imag = np.cos(angle), -np.sin(angle)
+    imag[0] = np.cos(np.pi * np.arange(points))
+    there = np.concatenate([real, imag])[:, :length]
+    weight = np.full((2 * length, 1), 2.0 / points)
+    weight[0] = weight[length] = 1.0 / points
+    back = (np.concatenate([real, imag]) * weight)[:, length:].T
+
+    def parts(table):
+        table = table.astype(np.float32)
+        high = table.astype(jnp.bfloat16)
+        return np.concatenate([high, (table - high.astype(np.float32)).astype(jnp.bfloat16)])
+
+    return parts(there), parts(back)
+
+
+def times(table, values):
+    both = jnp.dot(table, values, preferred_element_type=F32)
+    half = both.shape[0] // 2
+    return both[:half] + both[half:]
+
+
+def side_by_side(ref):
+    return jnp.concatenate([ref[tile].astype(BF16) for tile in range(ref.shape[0])], axis=1)
 
 
 def decayed_sums(starts, decay, blocks):
@@ -84,13 +101,19 @@
     return out
 
 
-def own_filter_kernel(product_ref, taps_ref, taps_out, part_out, signal_ref):
+def own_filter_kernel(product_ref, taps_ref, there_ref, wave_out, part_out, signal_ref, taps_out):
     tiles, length = product_ref.shape[0], product_ref.shape[1]
     blocks = length // ROWS
     signal_ref[:, pl.ds(0, ROWS), :] = jnp.zeros((tiles, ROWS, LANES), F32)
     for tile in range(tiles):
         signal_ref[tile, pl.ds(ROWS, length), :] = product_ref[tile].astype(F32)
         taps_out[tile] = turned(taps_ref[pl.ds(tile * LANES, LANES), :])
+    wave = times(there_ref[...], side_by_side(taps_out))
+    real, imag = wave[:length], wave[length:]
+    top = lax.broadcasted_iota(jnp.int32, real.shape, 0) == 0
+    wave_out[0] = real
+    wave_out[1] = jnp.where(top, 0.0, imag)
+    wave_out[2] = jnp.where(top, imag, real)
 
     def one_tile(tile, carry):
         sums = own_taps(signal_ref, taps_out, tile, blocks)
@@ -109,26 +132,32 @@
 
 
 def mix_kernel(
-    halo_ref, part_ref, taps_ref, q_ref, k_ref, mode_ref,
+    halo_ref, part_ref, wave_ref, there_ref, back_ref, q_ref, k_ref, mode_ref,
     one_out, mixed_out, state_out,
-    signal_ref,
+    earlier_ref,
 ):
     tiles, length = part_ref.shape[0], part_ref.shape[1]
     blocks = length // ROWS
     modes = state_out.shape[1] // tiles
-    signal_ref[:, pl.ds(length, ROWS), :] = jnp.zeros((tiles, ROWS, LANES), F32)
+    wave = times(there_ref[...], side_by_side(halo_ref))
+    real, imag = wave[:length], wave[length:]
+    made = jnp.concatenate(
+        [real * wave_ref[0] - imag * wave_ref[1], real * wave_ref[1] + imag * wave_ref[2]], axis=0
+    )
+    high = made.astype(BF16)
+    low = (made - high.astype(F32)).astype(BF16)
+    earlier_ref[...] = times(back_ref[...], high) + jnp.dot(
+        back_ref[pl.ds(0, length), :], low, preferred_element_type=F32
+    )
+
+    left = (ROWS - 1 - lax.broadcasted_iota(jnp.int32, (ROWS, LANES), 0)).astype(F32)
+
     for tile in range(tiles):
-        signal_ref[tile, pl.ds(0, length), :] = halo_ref[tile].astype(F32)
-
-    left = (ROWS - 1 - lax.broadcasted_iota(jnp.int32, (ROWS, LANES), 0)).astype(F32)
-
-    def one_tile(tile, carry):
-        sums = [rows_of(part_ref, tile, ROWS * at) for at in range(blocks)]
-        sums = earlier_taps(sums, signal_ref, taps_ref, tile, blocks)
         mixed = []
         for at in range(blocks):
             rows = pl.ds(ROWS * at, ROWS)
-            first = (q_ref[tile, rows, :] * sums[at]).astype(BF16).astype(F32)
+            summed = part_ref[tile, rows, :] + earlier_ref[rows, pl.ds(tile * LANES, LANES)]
+            first = (q_ref[tile, rows, :] * summed).astype(BF16).astype(F32)
             mixed.append((k_ref[tile, rows, :] * first).astype(BF16).astype(F32))
             one_out[tile, rows, :] = first
             mixed_out[tile, rows, :] = mixed[-1]
@@ -142,10 +171,7 @@
             found.append(jnp.sum(held * jnp.exp(-rate * left), axis=0, keepdims=True))
         state = jnp.concatenate(found, axis=0).astype(BF16)
         for peer in range(state_out.shape[0]):
-            state_out[peer, pl.ds(pl.multiple_of(tile * modes, modes), modes), :] = state
-        return carry
-
-    lax.fori_loop(0, tiles, one_tile, 0)
+            state_out[peer, pl.ds(tile * modes, modes), :] = state
 
 
 def local_conv(first, count, mixed_ref, mode_ref, conv_out, signal_ref, filter_ref):
@@ -266,11 +292,16 @@
     )(k_one, v_one, residues.T, decays.T, skip_gain.reshape(tiles, LANES))
     halo = lax.ppermute(product, seq, [(at, at + 1) for at in range(count - 1)])
     padded = pltpu.VMEM((tiles, length + ROWS, LANES), F32)
-    taps, part = call(own_filter_kernel, (wide, wide), (padded,))(*near_by(product, fir_taps))
+    there, back = (jnp.asarray(table) for table in spectrum_tables(length))
+    waves = array(F32, 3, length, channels)
+    wave, part = call(own_filter_kernel, (waves, wide), (padded, pltpu.VMEM((tiles, length, LANES), F32)))(
+        *near_by(product, fir_taps, there)
+    )
     q_turned, k_turned = call(turn_kernel, (wide, wide))(*near_by(q_one, k_two))
     one_turned, mixed, state = call(
-        mix_kernel, (wide, wide, array(BF16, mates, states, LANES)), (padded,)
-    )(*near_by(halo, part, taps, q_turned, k_turned, mode_rows))
+        mix_kernel, (wide, wide, array(BF16, mates, states, LANES)),
+        (pltpu.VMEM((length, channels), F32),),
+    )(*near_by(halo, part, wave, there, back, q_turned, k_turned, mode_rows))
     heard = lax.all_to_all(state, ("line", "core"), split_axis=0, concat_axis=0, tiled=True)
     early = tiles // 2
     held = array(F32, early, length, LANES)

time: 49.3 us -> 51.5 us (1.045)
  local copies, waits for them, and re-layouts: 0.02 us -> 4.03 us
  Pallas kernels: 9.09 us -> 7.36 us
    unnamed x8 -> x22, local copies, waits for them, and re-layouts: 0.02 us -> 4.03 us
    pallas_call x1, Pallas kernels: 1.13 us -> 0.11 us  [body(): call(product_kernel, (array(BF16, tiles, length, LANES), array(F32, tiles...]
    pallas_call x2, Pallas kernels: 3.68 us -> 2.98 us  [the longest x1 1.94 us: body(): call(own_filter_kernel, (waves, wide), (padded, pltpu.VMEM((tiles, length...]
where the time goes in v4:
time: 51.5 us; the launch traced here: 51.1 us
  blocking collectives  26.6 us (52%)
  Pallas kernels  7.36 us (14%)
  waiting for transfers between devices  6.81 us (13%)
  starting transfers between devices  5.47 us (11%)
  local copies, waits for them, and re-layouts  4.03 us (8%)
  between operations  0.77 us (1%)
    all_to_all x1, blocking collectives, body(): lax.all_to_all(state, ('line', 'core'), split_axis=0, concat_axis=0, tile...  26.6 us
    all_to_all x1, waiting for transfers between devices, body(): lax.all_to_all(whole, 'ring', split_axis=0, concat_axis=0, tiled=True)  6.81 us
    unnamed x22, local copies, waits for them, and re-layouts  4.03 us
    all_to_all x1, starting transfers between devices, body(): lax.all_to_all(whole, 'ring', split_axis=0, concat_axis=0, tiled=True)  3.59 us
    pallas_call x1, Pallas kernels, body(): call(own_filter_kernel, (waves, wide), (padded, pltpu.VMEM((tiles, length...  1.94 us
    ppermute x1, starting transfers between devices, body(): halo = lax.ppermute(product, seq, [(at, at + 1) for at in range(count - 1)])  1.88 us
    pallas_call x1, Pallas kernels, body(): call(last_local_kernel, (held, jax.ShapeDtypeStruct((channels, length), B...  1.51 us
    pallas_call x1, Pallas kernels, body(): call(finish_kernel, jax.ShapeDtypeStruct((channels, length), BF16))  1.15 us
  transfers between devices with their start and end apart: 2, of which 1 were waited for; matrix products, arithmetic and copies ran while one was open for 0% of the time, Pallas kernels for 8%

profile of v4, /device:TPU:112, one launch (start us, length us, event | category | flops | bytes accessed | tf_op | source)
XLA Modules:
  0.0 51.1 jit_solution(8946323488247917348)
XLA Ops:
  0.6 0.0 copy-start.10
  0.6 0.7 %copy-done.10 = f32[512]{0:T(512)S(1)} copy-done((f32[512]{0:T(512)S(1)}, f32[512]{0:T(512)}, u32[]{:S(2)}) %copy-start.10) | copy-done | bytes 2072
  1.3 0.0 copy-start.3
  1.3 0.9 %copy-done.3 = bf16[512,128]{1,0:T(8,128)(2,1)S(1)} copy-done((bf16[512,128]{1,0:T(8,128)(2,1)S(1)}, bf16[512,128]{1,0:T(8,128)(2,1)}, u32[]{:S(2)}) %copy-start.3) | copy-done | bytes 131096
  2.2 0.0 copy-start.4
  2.2 0.9 %copy-done.4 = bf16[512,128]{1,0:T(8,128)(2,1)S(1)} copy-done((bf16[512,128]{1,0:T(8,128)(2,1)S(1)}, bf16[512,128]{1,0:T(8,128)(2,1)}, u32[]{:S(2)}) %copy-start.4) | copy-done | bytes 131096
  3.1 0.0 copy-start.8
  3.1 0.8 %copy-done.8 = f32[512,16]{0,1:T(8,128)S(1)} copy-done((f32[512,16]{0,1:T(8,128)S(1)}, f32[512,16]{0,1:T(8,128)}, u32[]{:S(2)}) %copy-start.8) | copy-done | bytes 32792
  3.9 0.0 copy-start.9
  3.9 0.8 %copy-done.9 = f32[512,16]{0,1:T(8,128)S(1)} copy-done((f32[512,16]{0,1:T(8,128)S(1)}, f32[512,16]{0,1:T(8,128)}, u32[]{:S(2)}) %copy-start.9) | copy-done | bytes 32792
  4.6 0.0 copy-start.5
  4.6 0.0 copy-start.6
  4.6 0.1 shard_map.122
  4.8 0.0 copy-start
  4.8 0.0 copy-start.1
  4.8 1.9 %collective-permute-start = (bf16[4,128,128]{2,1,0:T(8,128)(2,1)S(1)}, bf16[4,128,128]{2,1,0:T(8,128)(2,1)S(1)}, u32[]{:S(2)}, u32[]{:S(2)}) collective-permute-start(bf16[4,128,128]{2,1,0:T(8,128)(2,1)S(1)} %get-tuple-element.15.product_ref), channel_id=1, source_target_pairs={{0,16},{16,32},{32,48},{48,64},{64,80},{80,96},{96,112},{112,128},... | collective-permute-start | bytes 393224 | tf_op jit(solution)/shard_map/ppermute | solution.py:293
  6.7 0.0 copy-done.5
  6.7 0.0 copy-done.6
  6.7 0.1 shard_map.124
  6.8 0.0 copy-done
  6.8 0.0 copy-done.1
  6.9 0.0 copy-start.2
  6.9 1.9 %shard_map.123 = (f32[3,128,512]{2,1,0:T(8,128)S(1)}, f32[4,128,128]{2,1,0:T(8,128)S(1)}) custom-call(bf16[4,128,128]{2,1,0:T(8,128)(2,1)S(1)} %get-tuple-element.15.product_ref, bf16[512,128]{1,0:T(8,128)(2,1)S(1)} %copy-done.1, bf16[512,128]{1,0:T(8,128)(2,1)S(1)} %copy-done), custom_call_target="tpu_custom_call" | custom-call | tf_op jit(solution)/shard_map/pallas_call | solution.py:297
  8.8 0.0 collective-permute-done.halo_ref
  8.8 0.0 copy-done.2
  8.8 1.0 %shard_map.125 = (f32[4,128,128]{2,1,0:T(8,128)S(1)}, f32[4,128,128]{2,1,0:T(8,128)S(1)}, bf16[8,64,128]{2,1,0:T(8,128)(2,1)S(1)}) custom-call(bf16[4,128,128]{2,1,0:T(8,128)(2,1)S(1)} %collective-permute-done.halo_ref, f32[4,128,128]{2,1,0:T(8,128)S(1)} %get-tuple-element.16.part_ref, f32[3,128,512]{2,1,0:T(8,128)S(1)} %get-tuple-element.17.wave_ref, ...), custom_call_target="tpu_custom_call" | custom-call | tf_op jit(solution)/shard_map/pallas_call | solution.py:301
  9.9 26.6 %all_to_all.10.heard_ref = bf16[8,64,128]{2,1,0:T(8,128)(2,1)S(1)} all-to-all(bf16[8,64,128]{2,1,0:T(8,128)(2,1)S(1)} %get-tuple-element.23), channel_id=1, replica_groups=mesh['line'=4,'ring'=8,'core'=2,'chan'=16] {'line','core'}, dimensions={0} | all-to-all | bytes 262144 | tf_op jit(solution)/shard_map/all_to_all | solution.py:305
  36.5 0.7 %shard_map.126 = (f32[64,128]{1,0:T(8,128)S(1)}, bf16[8,64,128]{2,1,0:T(8,128)(2,1)}) custom-call(bf16[8,64,128]{2,1,0:T(8,128)(2,1)S(1)} %all_to_all.10.heard_ref, f32[4,40,128]{2,1,0:T(8,128)S(1)} %get-tuple-element.20.mode_ref.conv_ref, f32[4,40,128]{2,1,0:T(8,128)S(1)} %get-tuple-element.20.mode_ref.conv_ref), custom_call_target="tpu_custom_call" | custom-call | tf_op jit(solution)/shard_map/pallas_call | solution.py:309
  37.2 3.6 %all-to-all-start.1 = ((bf16[8,64,128]{2,1,0:T(8,128)(2,1)}), bf16[8,64,128]{2,1,0:T(8,128)(2,1)S(1)}, u32[]{:S(2)}, u32[]{:S(2)}) async-start(bf16[8,64,128]{2,1,0:T(8,128)(2,1)} %get-tuple-element.26), calls=%async_computation.1 | async-start | bytes 262144 | tf_op jit(solution)/shard_map/all_to_all | solution.py:312
  40.8 0.7 %shard_map.128.early_ref = f32[2,128,128]{2,1,0:T(8,128)S(1)} custom-call(f32[4,128,128]{2,1,0:T(8,128)S(1)} %get-tuple-element.21.mixed_ref, f32[4,40,128]{2,1,0:T(8,128)S(1)} %get-tuple-element.20.mode_ref.conv_ref, f32[64,128]{1,0:T(8,128)S(1)} %get-tuple-element.24.before_ref), custom_call_target="tpu_custom_call" | custom-call | tf_op jit(solution)/shard_map/pallas_call | solution.py:313
  41.6 0.0 copy-start.7
  41.6 1.5 %shard_map.127 = (f32[2,128,128]{2,1,0:T(8,128)S(1)}, bf16[512,128]{1,0:T(8,128)(2,1)}) custom-call(f32[4,128,128]{2,1,0:T(8,128)S(1)} %get-tuple-element.21.mixed_ref, f32[4,40,128]{2,1,0:T(8,128)S(1)} %get-tuple-element.20.mode_ref.conv_ref, f32[4,128,128]{2,1,0:T(8,128)S(1)} %get-tuple-element.22.one_ref, f32[64,128]{1,0:T(8,128)S(1)} %get-tuple-element.24.before_ref), custom_call_target="tpu_custom_call" | custom-call | tf_op jit(solution)/shard_map/pallas_call | solution.py:314
  43.1 6.8 %all-to-all-done.1.heard_ref = bf16[8,64,128]{2,1,0:T(8,128)(2,1)S(1)} async-done(((bf16[8,64,128]{2,1,0:T(8,128)(2,1)}), bf16[8,64,128]{2,1,0:T(8,128)(2,1)S(1)}, u32[]{:S(2)}, u32[]{:S(2)}) %all-to-all-start.1) | async-done | bytes 131104 | tf_op jit(solution)/shard_map/all_to_all | solution.py:312
  49.9 0.0 copy-done.7
  49.9 1.2 %shard_map.129 = bf16[512,128]{1,0:T(8,128)(2,1)} custom-call(bf16[8,64,128]{2,1,0:T(8,128)(2,1)S(1)} %all-to-all-done.1.heard_ref, f32[64,128]{1,0:T(8,128)S(1)} %get-tuple-element.24.before_ref, f32[4,40,128]{2,1,0:T(8,128)S(1)} %get-tuple-element.20.mode_ref.conv_ref, f32[2,128,128]{2,1,0:T(8,128)S(1)} %shard_map.128.early_ref, ...), custom_call_target="tpu_custom_call" | custom-call | tf_op jit(solution)/shard_map/pallas_call | solution.py:317
Async XLA Ops:
  0.6 0.7 %copy-start.10 = (f32[512]{0:T(512)S(1)}, f32[512]{0:T(512)}, u32[]{:S(2)}) copy-start(f32[512]{0:T(512)} %param.19) | copy-start | bytes 6148
  1.3 0.9 %copy-start.3 = (bf16[512,128]{1,0:T(8,128)(2,1)S(1)}, bf16[512,128]{1,0:T(8,128)(2,1)}, u32[]{:S(2)}) copy-start(bf16[512,128]{1,0:T(8,128)(2,1)} %k_ref.2) | copy-start | bytes 393220
  2.2 0.9 %copy-start.4 = (bf16[512,128]{1,0:T(8,128)(2,1)S(1)}, bf16[512,128]{1,0:T(8,128)(2,1)}, u32[]{:S(2)}) copy-start(bf16[512,128]{1,0:T(8,128)(2,1)} %v_ref.1) | copy-start | bytes 393220
  3.1 0.8 %copy-start.8 = (f32[512,16]{0,1:T(8,128)S(1)}, f32[512,16]{0,1:T(8,128)}, u32[]{:S(2)}) copy-start(f32[512,16]{0,1:T(8,128)} %param.17) | copy-start | bytes 98308
  3.9 0.8 %copy-start.9 = (f32[512,16]{0,1:T(8,128)S(1)}, f32[512,16]{0,1:T(8,128)}, u32[]{:S(2)}) copy-start(f32[512,16]{0,1:T(8,128)} %param.18) | copy-start | bytes 98308
  4.6 2.0 %copy-start.5 = (bf16[512,128]{1,0:T(8,128)(2,1)S(1)}, bf16[512,128]{1,0:T(8,128)(2,1)}, u32[]{:S(2)}) copy-start(bf16[512,128]{1,0:T(8,128)(2,1)} %q_ref.1) | copy-start | bytes 393220
  4.6 2.0 %copy-start.6 = (bf16[512,128]{1,0:T(8,128)(2,1)S(1)}, bf16[512,128]{1,0:T(8,128)(2,1)}, u32[]{:S(2)}) copy-start(bf16[512,128]{1,0:T(8,128)(2,1)} %k_ref.3) | copy-start | bytes 393220
  4.8 2.1 %copy-start = (bf16[512,128]{1,0:T(8,128)(2,1)S(1)}, bf16[512,128]{1,0:T(8,128)(2,1)}, u32[]{:S(2)}) copy-start(bf16[512,128]{1,0:T(8,128)(2,1)} %constant.4.clone.there_ref) | copy-start | bytes 393220
  4.8 2.1 %copy-start.1 = (bf16[512,128]{1,0:T(8,128)(2,1)S(1)}, bf16[512,128]{1,0:T(8,128)(2,1)}, u32[]{:S(2)}) copy-start(bf16[512,128]{1,0:T(8,128)(2,1)} %taps_ref.1) | copy-start | bytes 393220
  4.8 4.0 %collective-permute-start = (bf16[4,128,128]{2,1,0:T(8,128)(2,1)S(1)}, bf16[4,128,128]{2,1,0:T(8,128)(2,1)S(1)}, u32[]{:S(2)}, u32[]{:S(2)}) collective-permute-start(bf16[4,128,128]{2,1,0:T(8,128)(2,1)S(1)} %get-tuple-element.15.product_ref), channel_id=1, source_target_pairs={{0,16},{16,32},{32,48},{48,64},{64,80},{80,96},{96,112},{112,128},... | collective-permute-start | bytes 393224 | tf_op jit(solution)/shard_map/ppermute | solution.py:293
  6.9 2.0 %copy-start.2 = (bf16[256,256]{1,0:T(8,128)(2,1)S(1)}, bf16[256,256]{1,0:T(8,128)(2,1)}, u32[]{:S(2)}) copy-start(bf16[256,256]{1,0:T(8,128)(2,1)} %constant.5.clone.back_ref) | copy-start | bytes 393220
  37.2 12.7 %all-to-all-start.1 = ((bf16[8,64,128]{2,1,0:T(8,128)(2,1)}), bf16[8,64,128]{2,1,0:T(8,128)(2,1)S(1)}, u32[]{:S(2)}, u32[]{:S(2)}) async-start(bf16[8,64,128]{2,1,0:T(8,128)(2,1)} %get-tuple-element.26), calls=%async_computation.1 | async-start | bytes 262144 | tf_op jit(solution)/shard_map/all_to_all | solution.py:312
  41.6 8.3 %copy-start.7 = (bf16[512,128]{1,0:T(8,128)(2,1)S(1)}, bf16[512,128]{1,0:T(8,128)(2,1)}, u32[]{:S(2)}) copy-start(bf16[512,128]{1,0:T(8,128)(2,1)} %gate_ref.1) | copy-start | bytes 393220
